TPU v7x, 256 devices: a whole 4x4x8 slice. The times are simulated.
256 devices in a mesh: dp: 8 (over x, core), expert: 8 (over z), mp: 4 (over y).
Axes of the slice: x: 4, y: 4, z: 8, core: 2. Of those that a mesh axis runs over, the one named last changes fastest.
Arguments:
- tokens: bfloat16 [8192, 3072], P(('dp', 'expert'), 'mp'), may hold values from -6 to 6
- expert_ids: int32 [8192, 2], P(('dp', 'expert')), may hold values from 0 to 7, all different within a row; in each aligned block of 128 rows (0 to 127, 128 to 255, ...) at most 36 rows name the same one
- route_weight: bfloat16 [8192, 2], P(('dp', 'expert')), may hold values from 0.099609375 to 1
- w_gate: bfloat16 [8, 3072, 8192], P(None, ('dp', 'expert'), 'mp'), may hold values from -0.109375 to 0.109375
- w_up: bfloat16 [8, 3072, 8192], P(None, ('dp', 'expert'), 'mp'), may hold values from -0.109375 to 0.109375
- grad_hidden: bfloat16 [8, 8, 8, 36, 8192], P('expert', 'dp', None, None, 'mp'), may hold values from -6 to 6
Outputs:
- hidden_out: bfloat16 [8, 8, 8, 36, 8192], P('expert', 'dp', None, None, 'mp')
- grad_tokens: bfloat16 [8192, 3072], P(('dp', 'expert'), 'mp')
Inputs may be any that keep to these rules, and one draw needn't show every extreme that they name: `expert_ids`: each row names 2 different experts; among the rows of one token group no expert is named more than 36 times, a bound that some block reaches.
All inputs are finite; a program needn't handle non-finite values.
Results may differ from a plain program's by a relative error of at most 0.0049.
Values may be sent and summed in bfloat16 or wider, within the bound.
A program may use at most 128 MiB of HBM per device.

v0:
```python
import math

import jax
import jax.numpy as jnp
from jax import lax
from jax.sharding import PartitionSpec as P

D = 3072


def sent_together(arrays, axis, split_dim, concat_dim, along):
    widths = [math.prod(a.shape[along:]) for a in arrays]
    both = jnp.concatenate(
        [a.reshape(*a.shape[:along], w) for a, w in zip(arrays, widths)], axis=along
    )
    result = lax.all_to_all(both, axis, split_axis=split_dim, concat_axis=concat_dim, tiled=True)
    pieces = jnp.split(result, [sum(widths[:k]) for k in range(1, len(widths))], axis=along)
    return tuple(
        (b.reshape(*result.shape[:along], *a.shape[along:]) for a, b in zip(arrays, pieces))
    )


def copy_for_each(shard, axis):
    copies = jnp.broadcast_to(shard, (lax.axis_size(axis), *shard.shape))
    return lax.all_to_all(copies, axis, split_axis=0, concat_axis=0, tiled=True)


def joined_along(pieces, dim):
    dims = list(pieces.shape[1:])
    dims[dim] *= pieces.shape[0]
    return jnp.moveaxis(pieces, 0, dim).reshape(dims)


def collect(shard, axis, dim):
    pieces = copy_for_each(shard, axis)
    return joined_along(pieces, dim)


def in_one_piece(arrays, axis, split_dim, concat_dim, along):
    widths = [a.shape[along] for a in arrays]
    both = jnp.concatenate(arrays, axis=along)
    result = lax.all_to_all(both, axis, split_axis=split_dim, concat_axis=concat_dim, tiled=True)
    return tuple(jnp.split(result, [sum(widths[:k]) for k in range(1, len(widths))], axis=along))


def sent_together_2(arrays, axis, dim, along):
    ends, at = ([], 0)
    for a in arrays[:-1]:
        at += a.shape[along]
        ends.append(at)
    both = jnp.concatenate(arrays, axis=along)
    return tuple(jnp.split(lax.all_gather(both, axis, axis=dim, tiled=True), ends, axis=along))


def slot_map(expert_ids, n_expert, slots_cap):
    flat_ids = expert_ids.reshape(-1)
    onehot = (flat_ids[:, None] == jnp.arange(n_expert, dtype=jnp.int32)[None, :]).astype(jnp.int32)
    before = jnp.cumsum(onehot, axis=0) - onehot
    position = jnp.sum(before * onehot, axis=1)
    target = flat_ids * slots_cap + position
    placed = target[:, None] == jnp.arange(n_expert * slots_cap, dtype=jnp.int32)[None, :]
    return placed.reshape(expert_ids.shape[0], expert_ids.shape[1], n_expert * slots_cap)


def per_device(tokens, expert_ids, route_weight, w_gate, w_up, grad_hidden):
    n_expert = lax.axis_size("expert")
    slots_cap = grad_hidden.shape[3]
    feat_part = tokens.shape[1]
    hidden_part = w_gate.shape[2]
    slot_count = n_expert * slots_cap
    placed = slot_map(expert_ids, n_expert, slots_cap).astype(jnp.float32)
    select = jnp.sum(placed, axis=1)
    sent_rows = jnp.dot(
        select.T.astype(jnp.bfloat16), tokens, preferred_element_type=jnp.float32
    ).astype(jnp.bfloat16)
    sent_scale = jnp.einsum(
        "tks,tk->s", placed, route_weight.astype(jnp.float32), precision=lax.Precision.HIGHEST
    ).astype(jnp.bfloat16)
    recv_rows, recv_scale = sent_together(
        (
            sent_rows.reshape(n_expert, slots_cap, feat_part),
            sent_scale.reshape(n_expert, slots_cap),
        ),
        "expert",
        0,
        0,
        2,
    )
    rows_full = collect(recv_rows, "mp", 2).reshape(slot_count, D)
    owned_gate, owned_up = in_one_piece((w_gate, w_up), "expert", 0, 1, 2)
    pieces = sent_together_2((owned_gate, owned_up), "dp", 1, 0)
    piece_gate = pieces[0][0]
    piece_up = pieces[1][0]
    gate_acc = jnp.dot(rows_full, piece_gate, preferred_element_type=jnp.float32)
    up_acc = jnp.dot(rows_full, piece_up, preferred_element_type=jnp.float32)
    weight = recv_scale.reshape(slot_count).astype(jnp.float32)[:, None]
    sigmoid_gate = jax.nn.sigmoid(gate_acc)
    hidden = (weight * gate_acc * sigmoid_gate * up_acc).astype(jnp.bfloat16)
    grad_act = weight * grad_hidden.reshape(slot_count, hidden_part).astype(jnp.float32)
    gate_grad = (grad_act * up_acc * sigmoid_gate * (1.0 + gate_acc * (1.0 - sigmoid_gate))).astype(
        jnp.bfloat16
    )
    up_grad = (grad_act * gate_acc * sigmoid_gate).astype(jnp.bfloat16)
    dims = (((1,), (1,)), ((), ()))
    back_term = lax.dot_general(gate_grad, piece_gate, dims, preferred_element_type=jnp.float32)
    back_term = back_term + lax.dot_general(
        up_grad, piece_up, dims, preferred_element_type=jnp.float32
    )
    shared = lax.psum_scatter(
        back_term.reshape(n_expert, slots_cap, D), "mp", scatter_dimension=2, tiled=True
    )
    returned = lax.all_to_all(shared, "expert", split_axis=0, concat_axis=0, tiled=True)
    grad_tokens = jnp.dot(
        select, returned.reshape(slot_count, feat_part), precision=lax.Precision.HIGHEST
    )
    hidden_out = hidden.reshape(1, 1, n_expert, slots_cap, hidden_part)
    return (hidden_out, grad_tokens.astype(jnp.bfloat16))


def solution(mesh):
    in_specs = (
        P(("dp", "expert"), "mp"),
        P(("dp", "expert"), None),
        P(("dp", "expert"), None),
        P(None, ("dp", "expert"), "mp"),
        P(None, ("dp", "expert"), "mp"),
        P("expert", "dp", None, None, "mp"),
    )
    out_specs = (P("expert", "dp", None, None, "mp"), P(("dp", "expert"), "mp"))
    return jax.shard_map(
        per_device, mesh=mesh, in_specs=in_specs, out_specs=out_specs, check_vma=False
    )
```

profile of v0, /device:TPU:1, one launch (start us, length us, event | category | flops | bytes accessed | tf_op | source)
XLA Modules:
  0.0 349.4 jit_solution(6983048578622911769)
XLA Ops:
  7.2 2.3 pad_maximum_fusion
  9.5 81.1 %all_to_all.27 = bf16[8,48,4096]{2,1,0:T(8,128)(2,1)S(1)} all-to-all(bf16[8,48,4096]{2,1,0:T(8,128)(2,1)S(1)} %pad_maximum_fusion), channel_id=1, replica_groups=mesh['dp'=8,'expert'=8,'mp'=4] {'expert'}, dimensions={0} | all-to-all | bytes 6291456 | tf_op jit(solution)/shard_map/all_to_all | solution.py:42
  90.6 0.4 fusion.16
  91.0 2.0 pad_maximum_fusion.1
  93.0 0.7 copy-done.5
  94.1 0.6 reduce-window.6
  94.7 0.2 slice_reduce_fusion
  95.0 0.1 reduce_sum.21
  95.2 0.2 convolution_reduce_fusion
  95.5 0.3 reshape_reshape.9
  95.8 0.7 copy-done.3
  96.4 0.3 convolution_convert_fusion
  96.8 17.9 %all_to_all.28 = bf16[8,36,769]{2,1,0:T(8,128)(2,1)S(1)} all-to-all(bf16[8,36,769]{2,1,0:T(8,128)(2,1)S(1)} %pad_maximum_fusion.2), channel_id=1, replica_groups=mesh['dp'=8,'expert'=8,'mp'=4] {'expert'}, dimensions={0} | all-to-all | bytes 885888 | tf_op jit(solution)/shard_map/all_to_all | solution.py:16
  114.8 1.3 broadcast_in_dim.2
  116.2 4.4 %all-to-all-start.1 = ((bf16[4,8,36,768]{3,1,2,0:T(8,128)(2,1)}), bf16[4,8,36,768]{3,1,2,0:T(8,128)(2,1)}, u32[]{:S(2)}, u32[]{:S(2)}) async-start(bf16[4,8,36,768]{3,1,2,0:T(8,128)(2,1)} %broadcast_in_dim.2), calls=%async_computation.1 | async-start | bytes 3538944 | tf_op jit(solution)/shard_map/all_to_all | solution.py:25
  120.6 2.0 copy.51
  122.6 1.6 reshape.70
  124.4 15.0 %all-to-all-done.1 = bf16[4,8,36,768]{3,1,2,0:T(8,128)(2,1)} async-done(((bf16[4,8,36,768]{3,1,2,0:T(8,128)(2,1)}), bf16[4,8,36,768]{3,1,2,0:T(8,128)(2,1)}, u32[]{:S(2)}, u32[]{:S(2)}) %all-to-all-start.1) | async-done | bytes 1769504 | tf_op jit(solution)/shard_map/all_to_all | solution.py:25
  139.4 2.9 copy.50
  142.3 0.3 copy.54
  142.6 71.8 %all-gather.2.cloned.1.call-done = bf16[2,3072,2048]{2,1,0:T(8,128)(2,1)} async-done(((bf16[2,384,2048]{2,1,0:T(8,128)(2,1)}), bf16[2,3072,2048]{2,1,0:T(8,128)(2,1)}) %all-gather.2.cloned.1.call-update) | async-done | bytes 25165840 | tf_op jit(solution)/shard_map/all_gather | solution.py:52
  214.3 7.0 %fusion.1 = f32[288,2048]{1,0:T(8,128)S(1)} fusion(bf16[288,3072]{1,0:T(8,128)(2,1)S(1)} %bitcast.33, bf16[2,3072,2048]{2,1,0:T(8,128)(2,1)} %all-gather.2.cloned.1.call-done), kind=kOutput, calls=%fused_computation.3 | convolution fusion | flops 3623878656 | bytes 16711680 | tf_op jit(solution)/shard_map/dot_general | solution.py:94
  221.3 11.3 %multiply_convert_fusion.2 = (bf16[288,2048]{1,0:T(8,128)(2,1)}, f32[288,2048]{1,0:T(8,128)}) fusion(f32[288,2048]{1,0:T(8,128)S(1)} %fusion.1, f32[288]{0:T(512)S(1)} %reshape.69, bf16[288,3072]{1,0:T(8,128)(2,1)S(1)} %bitcast.34, bf16[2,3072,2048]{2,1,0:T(8,128)(2,1)} %all-gather.2.cloned.1.call-done), kind=kOutput, calls=%fused_computation.11 | convolution fusion | flops 3628007424 | bytes 20251776 | tf_op jit(solution)/shard_map/dot_general | solution.py:95
  232.6 12.5 %fusion = f32[288,3072]{1,0:T(8,128)} fusion(bf16[2,3072,2048]{2,1,0:T(8,128)(2,1)} %all-gather.2.cloned.1.call-done, f32[288,2048]{1,0:T(8,128)} %copy-done.7, f32[288,2048]{1,0:T(8,128)} %get-tuple-element.17, f32[288,2048]{1,0:T(8,128)S(1)} %copy-done.2, f32[288]{0:T(512)S(1)} %reshape.69), kind=kOutput, calls=%fused_computation.2 | convolution fusion | flops 3630366720 | bytes 23200896 | tf_op jit(solution)/shard_map/dot_general | solution.py:105
  245.2 11.2 %fusion.4 = f32[288,3072]{1,0:T(8,128)S(1)} fusion(f32[288,3072]{1,0:T(8,128)} %fusion, bf16[2,3072,2048]{2,1,0:T(8,128)(2,1)} %all-gather.2.cloned.1.call-done, f32[288,2048]{1,0:T(8,128)} %copy-done.7, f32[288,2048]{1,0:T(8,128)} %reshape.70, f32[288]{0:T(512)S(1)} %reshape.69), kind=kOutput, calls=%fused_computation.6 | convolution fusion | flops 3628892160 | bytes 24380544 | tf_op jit(solution)/shard_map/dot_general | solution.py:106
  256.4 2.1 reshape.67
  258.5 48.0 %reduce-scatter.2.cloned.1.call-done = f32[8,36,768]{2,1,0:T(8,128)} async-done(((f32[8,36,3072]{2,1,0:T(8,128)}), f32[8,36,768]{2,1,0:T(8,128)}) %reduce-scatter.2.cloned.1.call-update) | async-done | bytes 884752 | tf_op jit(solution)/shard_map/reduce_scatter | solution.py:109
  306.5 6.7 %all-to-all-start.3 = ((f32[8,36,768]{2,1,0:T(8,128)}), f32[8,36,768]{2,1,0:T(8,128)S(1)}, u32[]{:S(2)}, u32[]{:S(2)}) async-start(f32[8,36,768]{2,1,0:T(8,128)} %reduce-scatter.2.cloned.1.call-done), calls=%async_computation.4 | async-start | bytes 1966080 | tf_op jit(solution)/shard_map/all_to_all | solution.py:112
  313.2 1.4 reshape.66
  314.6 1.7 copy.52
  316.3 24.7 %all-to-all-done.3 = f32[8,36,768]{2,1,0:T(8,128)S(1)} async-done(((f32[8,36,768]{2,1,0:T(8,128)}), f32[8,36,768]{2,1,0:T(8,128)S(1)}, u32[]{:S(2)}, u32[]{:S(2)}) %all-to-all-start.3) | async-done | bytes 884768 | tf_op jit(solution)/shard_map/all_to_all | solution.py:112
  341.1 1.5 convolution_convert_fusion.1
  (35 shorter events, 1.3 us)
Async XLA Ops:
  7.2 89.3 %copy-start = (bf16[128,768]{1,0:T(8,128)(2,1)S(1)}, bf16[128,768]{1,0:T(8,128)(2,1)}, u32[]{:S(2)}) copy-start(bf16[128,768]{1,0:T(8,128)(2,1)} %param.6) | copy-start | bytes 589828
  7.2 207.2 %all-gather.2.cloned.1.call-start = ((), (), s32[]{:S(2)}) async-start(), calls=%async_computation.5 | async-start | bytes 28311552 | tf_op jit(solution)/shard_map/all_gather | solution.py:52
  93.0 0.7 copy-start.5
  93.0 2.2 copy-start.6
  95.8 0.7 copy-start.3
  116.2 23.2 %all-to-all-start.1 = ((bf16[4,8,36,768]{3,1,2,0:T(8,128)(2,1)}), bf16[4,8,36,768]{3,1,2,0:T(8,128)(2,1)}, u32[]{:S(2)}, u32[]{:S(2)}) async-start(bf16[4,8,36,768]{3,1,2,0:T(8,128)(2,1)} %broadcast_in_dim.2), calls=%async_computation.1 | async-start | bytes 3538944 | tf_op jit(solution)/shard_map/all_to_all | solution.py:25
  120.5 185.9 %reduce-scatter.2.cloned.1.call-start = ((), (), s32[]{:S(2)}) async-start(), calls=%async_computation.6 | async-start | bytes 4915200 | tf_op jit(solution)/shard_map/reduce_scatter | solution.py:109
  221.3 11.3 %copy-start.7 = (f32[288,2048]{1,0:T(8,128)}, f32[288,2048]{1,0:T(8,128)S(1)}, u32[]{:S(2)}) copy-start(f32[288,2048]{1,0:T(8,128)S(1)} %fusion.1) | copy-start | bytes 7077892
  221.3 11.3 %copy-start.2 = (f32[288,2048]{1,0:T(8,128)S(1)}, f32[288,2048]{1,0:T(8,128)}, u32[]{:S(2)}) copy-start(f32[288,2048]{1,0:T(8,128)} %reshape.70) | copy-start | bytes 7077892
  306.5 34.5 %all-to-all-start.3 = ((f32[8,36,768]{2,1,0:T(8,128)}), f32[8,36,768]{2,1,0:T(8,128)S(1)}, u32[]{:S(2)}, u32[]{:S(2)}) async-start(f32[8,36,768]{2,1,0:T(8,128)} %reduce-scatter.2.cloned.1.call-done), calls=%async_computation.4 | async-start | bytes 1966080 | tf_op jit(solution)/shard_map/all_to_all | solution.py:112
  313.2 29.4 %copy-start.1 = (bf16[128,768]{1,0:T(8,128)(2,1)S(1)}, bf16[128,768]{1,0:T(8,128)(2,1)}, u32[]{:S(2)}) copy-start(bf16[128,768]{1,0:T(8,128)(2,1)} %param.6) | copy-start | bytes 589828
  314.6 26.5 %copy-start.4 = (f32[128,288]{0,1:T(8,128)S(1)}, f32[128,288]{0,1:T(8,128)}, u32[]{:S(2)}) copy-start(f32[128,288]{0,1:T(8,128)} %copy-done.3) | copy-start | bytes 442372
Sparse Core Ops, SparseCore 0:
  93.1 121.1 all-gather.1
  258.6 47.7 reduce-scatter.1
where the time goes:
time: 350 us; the launch traced here: 349 us
  waiting for transfers between devices  159 us (45%)
  blocking collectives  99 us (28%)
  matrix products  44 us (13%)
  local copies, waits for them, and re-layouts  16.4 us (5%)
  between operations  14.3 us (4%)
  starting transfers between devices  11.2 us (3%)
  other arithmetic  5.21 us (1%)
    all_to_all x1, blocking collectives, in_one_piece(): lax.all_to_all(both, axis, split_axis=split_dim, concat_axis=concat_dim,...  81.1 us
    all_gather x1, waiting for transfers between devices, sent_together_2(): lax.all_gather(both, axis, axis=dim, tiled=True)  71.8 us
    reduce_scatter x1, waiting for transfers between devices, per_device(): lax.psum_scatter(back_term.reshape(n_expert, slots_cap, D), 'mp', scatter...  48 us
    all_to_all x1, waiting for transfers between devices, per_device(): lax.all_to_all(shared, 'expert', split_axis=0, concat_axis=0, tiled=True)  24.7 us
    all_to_all x1, blocking collectives, sent_together(): lax.all_to_all(both, axis, split_axis=split_dim, concat_axis=concat_dim,...  17.9 us
    all_to_all x1, waiting for transfers between devices, copy_for_each(): return lax.all_to_all(copies, axis, split_axis=0, concat_axis=0, tiled=True)  15 us
    dot_general x1, matrix products, per_device(): lax.dot_general(gate_grad, piece_gate, dims, preferred_element_type=jnp.f...  12.5 us
    dot_general x1, matrix products, per_device(): up_acc = jnp.dot(rows_full, piece_up, preferred_element_type=jnp.float32)  11.3 us
  transfers between devices with their start and end apart: 4, of which 4 were waited for; matrix products, arithmetic and copies ran while one was open for 4% of the time, Pallas kernels for 0%

commit v1 on v0

v1 whole, which is shorter than its diff:
```python
import functools

import jax
import jax.numpy as jnp
from jax import lax
from jax.experimental import pallas as pl
from jax.experimental.pallas import tpu as pltpu
from jax.sharding import PartitionSpec as P

MESH = pl.DeviceIdType.MESH
UNITS = 128


def slot_map(expert_ids, n_expert, slots_cap):
    flat_ids = expert_ids.reshape(-1)
    onehot = (flat_ids[:, None] == jnp.arange(n_expert, dtype=jnp.int32)[None, :]).astype(jnp.int32)
    before = jnp.cumsum(onehot, axis=0) - onehot
    position = jnp.sum(before * onehot, axis=1)
    target = position * n_expert + flat_ids
    placed = target[:, None] == jnp.arange(n_expert * slots_cap, dtype=jnp.int32)[None, :]
    return placed.reshape(expert_ids.shape[0], expert_ids.shape[1], n_expert * slots_cap)


def stream_kernel(nx, nz, rows_hbm, scale_hbm, gate_hbm, up_hbm, grad_hbm, hid_hbm, back_hbm,
                  stage, wbuf, rows, scale, grad, hid, acc, bsend, brecv,
                  stage_sem, own_sem, z_send, z_recv, x_send, x_recv,
                  in_sem, in_send, in_recv, hid_sem, hid_send, hid_recv, b_send, b_recv, out_sem):
    dp, z, y = lax.axis_index("dp"), lax.axis_index("expert"), lax.axis_index("mp")
    x, c = dp // 2, lax.rem(dp, 2)
    other = 1 - c
    left, right = lax.rem(x + nx - 1, nx), lax.rem(x + 1, nx)
    far = lax.rem(x + 2, nx)
    chunks = wbuf.shape[0]
    part = gate_hbm.shape[1]
    own_rows = part * nz
    chip_rows = 2 * own_rows
    slots = rows.shape[1]
    half_units = chunks * UNITS

    barrier = pltpu.get_barrier_semaphore()
    peers = [(dp - c + cc, lax.rem(z + o, nz), y) for o in range(1, nz) for cc in (0, 1)]
    peers += [(dp - c + other, z, y), (left * 2 + c, z, y), (right * 2 + c, z, y)]
    for peer in peers:
        pl.semaphore_signal(barrier, inc=1, device_id=peer, device_id_type=MESH)

    def stage_copies(k):
        copies = []
        for cc in (0, 1):
            at = pl.multiple_of(cc * half_units + k * UNITS, UNITS)
            copies.append(pltpu.make_async_copy(
                gate_hbm.at[:, :, pl.ds(at, UNITS)], stage.at[k, cc, :, :, pl.ds(0, UNITS)], stage_sem.at[k]))
            copies.append(pltpu.make_async_copy(
                up_hbm.at[:, :, pl.ds(at, UNITS)], stage.at[k, cc, :, :, pl.ds(UNITS, UNITS)], stage_sem.at[k]))
        return copies

    def stage_start(k, _):
        for copy in stage_copies(k):
            copy.start()
        return 0

    lax.fori_loop(0, chunks, stage_start, 0)
    grad_cols = pl.ds(pl.multiple_of(c * half_units, half_units), half_units)
    grad_other = pl.ds(pl.multiple_of(other * half_units, half_units), half_units)
    local_in = [
        pltpu.make_async_copy(rows_hbm, rows.at[c], in_sem.at[0]),
        pltpu.make_async_copy(scale_hbm, scale.at[c], in_sem.at[1]),
        pltpu.make_async_copy(grad_hbm.at[:, grad_cols], grad.at[c], in_sem.at[2]),
    ]
    for copy in local_in:
        copy.start()

    pl.semaphore_wait(barrier, len(peers))

    partner = (dp - c + other, z, y)
    remote_in = [
        pltpu.make_async_remote_copy(rows_hbm, rows.at[c], in_send.at[0], in_recv.at[0], partner, MESH),
        pltpu.make_async_remote_copy(scale_hbm, scale.at[c], in_send.at[1], in_recv.at[1], partner, MESH),
        pltpu.make_async_remote_copy(grad_hbm.at[:, grad_other], grad.at[c], in_send.at[2], in_recv.at[2], partner, MESH),
    ]
    for copy in remote_in:
        copy.start()

    my_block = pl.ds(pl.multiple_of(x * chip_rows + c * own_rows + z * part, 16), part)
    offsets = []
    for o in range(1, nz // 2):
        offsets += [o, nz - o]
    offsets.append(nz // 2)

    def send_z(k, _):
        pltpu.make_async_copy(stage.at[k], stage.at[k], stage_sem.at[k]).wait()
        for o in offsets + [0]:
            zt = lax.rem(z + o, nz)
            for cc in ((c, other) if o else (other,)):
                pltpu.make_async_remote_copy(
                    stage.at[k, cc, zt], wbuf.at[k, my_block, :], z_send.at[k], z_recv.at[k],
                    (dp - c + cc, zt, y), MESH).start()
        pltpu.make_async_copy(stage.at[k, c, z], wbuf.at[k, my_block, :], own_sem.at[k]).start()
        return 0

    lax.fori_loop(0, chunks, send_z, 0)

    def rows_of(chip, first, count):
        return pl.ds(pl.multiple_of(chip * chip_rows + first, 16), count)

    def x_copy(k, way, chip, first, count):
        where = wbuf.at[k, rows_of(chip, first, count), :]
        to = right if way % 2 == 0 else left
        return pltpu.make_async_remote_copy(
            where, where, x_send.at[way, k], x_recv.at[way, k], (to * 2 + c, z, y), MESH)

    n_in = 2 * nz - 1

    def step_own(k):
        whole = wbuf.at[k, pl.ds(0, n_in * part), :]
        pltpu.make_async_copy(whole, whole, z_recv.at[k]).wait()
        pltpu.make_async_copy(stage.at[k, c, z], wbuf.at[k, my_block, :], own_sem.at[k]).wait()
        x_copy(k, 0, x, 0, chip_rows).start()
        x_copy(k, 1, x, 0, chip_rows).start()

    def step_relay(k):
        x_copy(k, 0, left, 0, chip_rows).wait_recv()
        x_copy(k, 2, left, 0, own_rows).start()
        x_copy(k, 1, right, 0, chip_rows).wait_recv()
        x_copy(k, 3, right, own_rows, own_rows).start()

    def hid_out(k):
        cols = pl.ds(pl.multiple_of(c * half_units + k * UNITS, UNITS), UNITS)
        here = pltpu.make_async_copy(hid.at[k, c], hid_hbm.at[:, cols], hid_sem.at[k])
        there = pltpu.make_async_remote_copy(
            hid.at[k, other], hid_hbm.at[:, cols], hid_send.at[k], hid_recv.at[k], partner, MESH)
        return here, there

    def compute(k):
        x_copy(k, 2, far, 0, own_rows).wait_recv()
        x_copy(k, 3, far, own_rows, own_rows).wait_recv()
        at = pl.ds(pl.multiple_of(k * UNITS, UNITS), UNITS)
        both = jnp.dot(rows[...].reshape(2 * slots, rows.shape[2]), wbuf[k], preferred_element_type=jnp.float32)
        gate, up = both[:, :UNITS], both[:, UNITS:]
        weight = scale[...].reshape(2 * slots, UNITS)
        sig = jax.nn.sigmoid(gate)
        hidden = (weight * gate * sig * up).astype(jnp.bfloat16)
        hid[k] = hidden.reshape(2, slots, UNITS)
        grad_act = weight * grad[:, :, at].reshape(2 * slots, UNITS).astype(jnp.float32)
        gate_grad = (grad_act * up * sig * (1.0 + gate * (1.0 - sig))).astype(jnp.bfloat16)
        up_grad = (grad_act * gate * sig).astype(jnp.bfloat16)
        pair = jnp.concatenate([gate_grad, up_grad], axis=1)
        here, there = hid_out(k)
        here.start()
        there.start()
        width = 768

        def back(n, _):
            cols = pl.ds(pl.multiple_of(n * width, width), width)
            term = lax.dot_general(pair, wbuf[k, cols, :], (((1,), (1,)), ((), ())),
                                   preferred_element_type=jnp.float32)
            term = term.reshape(2, slots, width)

            @pl.when(k == 0)
            def _():
                acc[:, :, cols] = term

            @pl.when(k > 0)
            def _():
                acc[:, :, cols] = acc[:, :, cols] + term
            return 0

        lax.fori_loop(0, acc.shape[2] // width, back, 0)

    step_own(0)
    step_own(1)
    step_relay(0)
    for copy in local_in:
        copy.wait()
    pltpu.make_async_copy(rows_hbm, rows.at[other], in_recv.at[0]).wait()
    pltpu.make_async_copy(scale_hbm, scale.at[other], in_recv.at[1]).wait()
    pltpu.make_async_copy(grad_hbm.at[:, grad_other], grad.at[other], in_recv.at[2]).wait()

    def main(k, _):
        @pl.when(k + 2 < chunks)
        def _():
            step_own(k + 2)

        @pl.when(k + 1 < chunks)
        def _():
            step_relay(k + 1)
        compute(k)
        return 0

    lax.fori_loop(0, chunks, main, 0)

    bsend[...] = acc[other].astype(jnp.bfloat16)
    swap = pltpu.make_async_remote_copy(bsend, brecv, b_send, b_recv, partner, MESH)
    swap.start()
    swap.wait()
    bsend[...] = (acc[c] + brecv[...].astype(jnp.float32)).astype(jnp.bfloat16)
    out = pltpu.make_async_copy(bsend, back_hbm, out_sem)
    out.start()

    for copy in remote_in:
        copy.wait_send()

    def drain(k, _):
        whole = wbuf.at[k, pl.ds(0, n_in * part), :]
        pltpu.make_async_copy(whole, whole, z_send.at[k]).wait()
        x_copy(k, 0, x, 0, chip_rows).wait_send()
        x_copy(k, 1, x, 0, chip_rows).wait_send()
        x_copy(k, 2, left, 0, own_rows).wait_send()
        x_copy(k, 3, right, own_rows, own_rows).wait_send()
        here, there = hid_out(k)
        here.wait()
        there.wait_send()
        cols = pl.ds(pl.multiple_of(other * half_units + k * UNITS, UNITS), UNITS)
        pltpu.make_async_copy(hid.at[k, other], hid_hbm.at[:, cols], hid_recv.at[k]).wait()
        return 0

    lax.fori_loop(0, chunks, drain, 0)
    out.wait()


def stream(nx, nz, rows, scale, w_gate, w_up, grad):
    slots, d = rows.shape
    hidden = grad.shape[1]
    chunks = hidden // 2 // UNITS
    part = w_gate.shape[1]
    bf16 = jnp.bfloat16
    dma = pltpu.SemaphoreType.DMA
    return pl.pallas_call(
        functools.partial(stream_kernel, nx, nz),
        out_shape=(jax.ShapeDtypeStruct((slots, hidden), bf16), jax.ShapeDtypeStruct((slots, d), bf16)),
        in_specs=[pl.BlockSpec(memory_space=pl.ANY)] * 5,
        out_specs=[pl.BlockSpec(memory_space=pl.ANY)] * 2,
        scratch_shapes=[
            pltpu.VMEM((chunks, 2, nz, part, 2 * UNITS), bf16),
            pltpu.VMEM((chunks, d, 2 * UNITS), bf16),
            pltpu.VMEM((2, slots, d), bf16),
            pltpu.VMEM((2, slots, UNITS), jnp.float32),
            pltpu.VMEM((2, slots, hidden // 2), bf16),
            pltpu.VMEM((chunks, 2, slots, UNITS), bf16),
            pltpu.VMEM((2, slots, d), jnp.float32),
            pltpu.VMEM((slots, d), bf16),
            pltpu.VMEM((slots, d), bf16),
            dma((chunks,)), dma((chunks,)), dma((chunks,)), dma((chunks,)), dma((4, chunks)), dma((4, chunks)),
            dma((3,)), dma((3,)), dma((3,)), dma((chunks,)), dma((chunks,)), dma((chunks,)), dma(()), dma(()), dma(()),
        ],
        compiler_params=pltpu.CompilerParams(
            collective_id=0, has_side_effects=True, vmem_limit_bytes=60 * 1024 * 1024),
        name="stream",
    )(rows, scale, w_gate, w_up, grad)


def per_device(nx, nz, tokens, expert_ids, route_weight, w_gate, w_up, grad_hidden):
    slots_cap = grad_hidden.shape[3]
    feat = tokens.shape[1]
    hidden_part = w_gate.shape[2]
    slots = nz * slots_cap
    placed = slot_map(expert_ids, nz, slots_cap).astype(jnp.float32)
    select = jnp.sum(placed, axis=1)
    sent_rows = jnp.dot(select.T.astype(jnp.bfloat16), tokens, preferred_element_type=jnp.float32).astype(jnp.bfloat16)
    sent_scale = jnp.einsum("tks,tk->s", placed, route_weight.astype(jnp.float32),
                            precision=lax.Precision.HIGHEST).astype(jnp.bfloat16)
    both = jnp.concatenate([sent_rows, jnp.broadcast_to(sent_scale[:, None], (slots, 128))], axis=1)
    both = both.reshape(slots_cap, nz, feat + 128).transpose(1, 0, 2)
    both = lax.all_to_all(both, "expert", split_axis=0, concat_axis=0, tiled=True)
    both = both.transpose(1, 0, 2).reshape(slots, feat + 128)
    scale = both[:, feat:].astype(jnp.float32)
    rows_full = lax.all_gather(both[:, :feat], "mp", axis=1, tiled=True)
    grad = grad_hidden.transpose(0, 1, 3, 2, 4).reshape(slots, hidden_part)
    hidden, back = stream(nx, nz, rows_full, scale, w_gate, w_up, grad)
    shared = lax.psum_scatter(back, "mp", scatter_dimension=1, tiled=True)
    shared = shared.reshape(slots_cap, nz, feat).transpose(1, 0, 2)
    returned = lax.all_to_all(shared, "expert", split_axis=0, concat_axis=0, tiled=True)
    returned = returned.transpose(1, 0, 2).reshape(slots, feat)
    grad_tokens = jnp.dot(select.astype(jnp.bfloat16), returned, preferred_element_type=jnp.float32)
    hidden_out = hidden.reshape(1, 1, slots_cap, nz, hidden_part).transpose(0, 1, 3, 2, 4)
    return hidden_out, grad_tokens.astype(jnp.bfloat16)


def solution(mesh):
    nx, nz = mesh.shape["dp"] // 2, mesh.shape["expert"]
    in_specs = (
        P(("dp", "expert"), "mp"),
        P(("dp", "expert"), None),
        P(("dp", "expert"), None),
        P(None, ("dp", "expert"), "mp"),
        P(None, ("dp", "expert"), "mp"),
        P("expert", "dp", None, None, "mp"),
    )
    out_specs = (P("expert", "dp", None, None, "mp"), P(("dp", "expert"), "mp"))
    return jax.shard_map(
        functools.partial(per_device, nx, nz), mesh=mesh, in_specs=in_specs, out_specs=out_specs, check_vma=False
    )
```

time: 350 us -> 260 us (0.74)
  Pallas kernels: 0 us -> 130 us
  waiting for transfers between devices: 159 us -> 73.3 us
  blocking collectives: 99 us -> 25.9 us
  matrix products: 44 us -> 2.07 us
  local copies, waits for them, and re-layouts: 16.4 us -> 5.42 us
  starting transfers between devices: 11.2 us -> 6.82 us
    pallas_call x0 -> x1, Pallas kernels: none -> 130 us  [stream(): pl.pallas_call(functools.partial(stream_kernel, nx, nz), out_shape=(jax.S...]
    all_to_all x2 -> x1, blocking collectives: 99 us -> 25.9 us  [per_device(): lax.all_to_all(both, 'expert', split_axis=0, concat_axis=0, tiled=True)]
    all_gather x1, waiting for transfers between devices: 71.8 us -> 28 us  [per_device(): rows_full = lax.all_gather(both[:, :feat], 'mp', axis=1, tiled=True)]
    dot_general x5 -> x1, matrix products: 43.5 us -> 0.97 us  [per_device(): jnp.dot(select.astype(jnp.bfloat16), returned, preferred_element_type=jnp...]
    reduce_scatter x1, waiting for transfers between devices: 48 us -> 28 us  [per_device(): shared = lax.psum_scatter(back, 'mp', scatter_dimension=1, tiled=True)]
    all_to_all x1 -> x0, waiting for transfers between devices: 15 us -> none  [copy_for_each(): return lax.all_to_all(copies, axis, split_axis=0, concat_axis=0, tiled=True)]
    all_to_all x1, waiting for transfers between devices: 24.7 us -> 17.2 us  [per_device(): lax.all_to_all(shared, 'expert', split_axis=0, concat_axis=0, tiled=True)]
    all_to_all x1 -> x0, starting transfers between devices: 4.38 us -> none  [copy_for_each(): return lax.all_to_all(copies, axis, split_axis=0, concat_axis=0, tiled=True)]
  transfers between devices with their start and end apart: 4 -> 3, of which waited for: 4 -> 3; matrix products, arithmetic and copies ran while one was open for 4% -> 0% of each run, Pallas kernels for 0% -> 0%
where the time goes in v1:
time: 260 us
  Pallas kernels  130 us (50%)
  waiting for transfers between devices  73.3 us (28%)
  blocking collectives  25.9 us (10%)
  between operations  14.2 us (5%)
  starting transfers between devices  6.82 us (3%)
  local copies, waits for them, and re-layouts  5.42 us (2%)
    pallas_call x1, Pallas kernels, stream(): pl.pallas_call(functools.partial(stream_kernel, nx, nz), out_shape=(jax.S...  130 us
    all_gather x1, waiting for transfers between devices, per_device(): rows_full = lax.all_gather(both[:, :feat], 'mp', axis=1, tiled=True)  28 us
    reduce_scatter x1, waiting for transfers between devices, per_device(): shared = lax.psum_scatter(back, 'mp', scatter_dimension=1, tiled=True)  28 us
    all_to_all x1, blocking collectives, per_device(): lax.all_to_all(both, 'expert', split_axis=0, concat_axis=0, tiled=True)  25.9 us
    all_to_all x1, waiting for transfers between devices, per_device(): lax.all_to_all(shared, 'expert', split_axis=0, concat_axis=0, tiled=True)  17.2 us
    all_to_all x1, starting transfers between devices, per_device(): lax.all_to_all(shared, 'expert', split_axis=0, concat_axis=0, tiled=True)  6.74 us
  transfers between devices with their start and end apart: 3, of which 3 were waited for; matrix products, arithmetic and copies ran while one was open for 0% of the time, Pallas kernels for 0%

profile of v1, /device:TPU:1, one launch (start us, length us, event | category | flops | bytes accessed | tf_op | source)
XLA Modules:
  0.0 259.6 jit_solution(369659439258989578)
XLA Ops:
  7.2 0.0 copy-start
  7.2 0.0 all-gather.2.cloned.1.call-start
  7.2 0.8 copy.33
  8.0 0.1 eq.43
  8.2 0.1 eq.39
  8.3 0.6 reduce-window.6
  8.9 0.2 slice_reduce_fusion
  9.2 0.1 fusion.6
  9.3 0.1 mul.19
  9.4 0.1 copy.35
  9.5 0.7 add.9
  10.2 0.9 convolution_reduce_fusion
  11.1 0.0 copy-done
  11.1 0.3 convolution_convert_fusion
  11.4 0.1 broadcast_in_dim.2
  11.5 0.1 copy.50
  11.6 25.9 %all_to_all.10 = bf16[8,36,896]{2,1,0:T(8,128)(2,1)S(1)} all-to-all(bf16[8,36,896]{2,1,0:T(8,128)(2,1)S(1)} %bitcast.36), channel_id=1, replica_groups=mesh['dp'=8,'expert'=8,'mp'=4] {'expert'}, dimensions={0} | all-to-all | bytes 1032192 | tf_op jit(solution)/shard_map/all_to_all | solution.py:263
  37.5 0.1 copy.51
  37.5 0.8 slice.17
  38.3 0.0 all-gather.2.cloned.1.call-update
  38.3 0.0 reduce-scatter.2.cloned.1.call-start
  38.4 0.7 slice_convert_fusion.scale_hbm
  39.1 28.0 %all-gather.2.cloned.1.call-done.rows_hbm = bf16[288,3072]{1,0:T(8,128)(2,1)} async-done(((bf16[288,768]{1,0:T(8,128)(2,1)}), bf16[288,3072]{1,0:T(8,128)(2,1)}) %all-gather.2.cloned.1.call-update) | async-done | bytes 1769488 | tf_op jit(solution)/shard_map/all_gather | solution.py:266
  67.1 129.8 %stream.1 = (bf16[288,2048]{1,0:T(8,128)(2,1)}, bf16[288,3072]{1,0:T(8,128)(2,1)}) custom-call(bf16[288,3072]{1,0:T(8,128)(2,1)} %all-gather.2.cloned.1.call-done.rows_hbm, f32[288,128]{1,0:T(8,128)} %slice_convert_fusion.scale_hbm, bf16[8,48,2048]{2,1,0:T(8,128)(2,1)} %gate_hbm.1, bf16[8,48,2048]{2,1,0:T(8,128)(2,1)} %up_hbm.1, bf16[288,2048]{1,0:T(8,128)(2,1)} %bitcast.41), custom_call_target="tpu_custom_call" | custom-call | tf_op jit(solution)/shard_map/stream/pallas_call | solution.py:227
  197.0 0.0 reduce-scatter.2.cloned.1.call-update
  197.0 0.0 copy-start.1
  197.0 28.0 %reduce-scatter.2.cloned.1.call-done = bf16[288,768]{1,0:T(8,128)(2,1)} async-done(((bf16[288,3072]{1,0:T(8,128)(2,1)}), bf16[288,768]{1,0:T(8,128)(2,1)}) %reduce-scatter.2.cloned.1.call-update) | async-done | bytes 442384 | tf_op jit(solution)/shard_map/reduce_scatter | solution.py:269
  225.0 1.9 copy.52
  226.8 6.7 %all-to-all-start.1 = ((bf16[8,36,768]{2,1,0:T(8,128)(2,1)}), bf16[8,36,768]{2,1,0:T(8,128)(2,1)S(1)}, u32[]{:S(2)}, u32[]{:S(2)}) async-start(bf16[8,36,768]{2,1,0:T(8,128)(2,1)} %bitcast.35), calls=%async_computation.2 | async-start | bytes 983040 | tf_op jit(solution)/shard_map/all_to_all | solution.py:271
  233.6 17.2 %all-to-all-done.1 = bf16[8,36,768]{2,1,0:T(8,128)(2,1)S(1)} async-done(((bf16[8,36,768]{2,1,0:T(8,128)(2,1)}), bf16[8,36,768]{2,1,0:T(8,128)(2,1)S(1)}, u32[]{:S(2)}, u32[]{:S(2)}) %all-to-all-start.1) | async-done | bytes 442400 | tf_op jit(solution)/shard_map/all_to_all | solution.py:271
  250.8 1.0 convolution_convert_fusion.1
  251.8 1.0 copy.54
  (7 shorter events, 0.1 us)
Async XLA Ops:
  7.2 3.9 %copy-start = (bf16[128,768]{1,0:T(8,128)(2,1)S(1)}, bf16[128,768]{1,0:T(8,128)(2,1)}, u32[]{:S(2)}) copy-start(bf16[128,768]{1,0:T(8,128)(2,1)} %param.6) | copy-start | bytes 589828
  7.2 59.9 %all-gather.2.cloned.1.call-start = ((), (), s32[]{:S(2)}) async-start(), calls=%async_computation.3 | async-start | bytes 2211840 | tf_op jit(solution)/shard_map/all_gather | solution.py:266
  38.3 186.6 %reduce-scatter.2.cloned.1.call-start = ((), (), s32[]{:S(2)}) async-start(), calls=%async_computation.4 | async-start | bytes 2211840 | tf_op jit(solution)/shard_map/reduce_scatter | solution.py:269
  197.0 54.8 %copy-start.1 = (bf16[288,2048]{1,0:T(8,128)(2,1)S(1)}, bf16[288,2048]{1,0:T(8,128)(2,1)}, u32[]{:S(2)}) copy-start(bf16[288,2048]{1,0:T(8,128)(2,1)} %get-tuple-element.4) | copy-start | bytes 3538948
  226.8 23.9 %all-to-all-start.1 = ((bf16[8,36,768]{2,1,0:T(8,128)(2,1)}), bf16[8,36,768]{2,1,0:T(8,128)(2,1)S(1)}, u32[]{:S(2)}, u32[]{:S(2)}) async-start(bf16[8,36,768]{2,1,0:T(8,128)(2,1)} %bitcast.35), calls=%async_computation.2 | async-start | bytes 983040 | tf_op jit(solution)/shard_map/all_to_all | solution.py:271
Sparse Core Ops, SparseCore 0:
  38.5 28.6 all-gather.1
  197.1 27.8 reduce-scatter.1

commit v2 on v1

v2 whole, which is shorter than its diff:
```python
import functools

import jax
import jax.numpy as jnp
from jax import lax
from jax.experimental import pallas as pl
from jax.experimental.pallas import tpu as pltpu
from jax.sharding import PartitionSpec as P

MESH = pl.DeviceIdType.MESH
UNITS = 128


def slot_map(expert_ids, n_expert, slots_cap):
    flat_ids = expert_ids.reshape(-1)
    onehot = (flat_ids[:, None] == jnp.arange(n_expert, dtype=jnp.int32)[None, :]).astype(jnp.int32)
    before = jnp.cumsum(onehot, axis=0) - onehot
    position = jnp.sum(before * onehot, axis=1)
    target = position * n_expert + flat_ids
    placed = target[:, None] == jnp.arange(n_expert * slots_cap, dtype=jnp.int32)[None, :]
    return placed.reshape(expert_ids.shape[0], expert_ids.shape[1], n_expert * slots_cap)


def stream_kernel(nx, nz, ny, select, planes_hbm, gate_hbm, up_hbm, grad_hbm, hid_hbm, tok_out,
                  stage, wbuf, planes, spread, rows, scale, grad, hid, acc, bsend, brecv, ysend, yrecv, final, zsend, back,
                  stage_sem, own_sem, z_send, z_recv, x_send, x_recv, tok_own, tok_send, tok_recv, y_send, y_recv,
                  in_sem, p_send, p_recv, hid_sem, hid_send, hid_recv, b_send, b_recv, ys_send, ys_recv,
                  r_own, r_send, r_recv):
    dp, z, y = lax.axis_index("dp"), lax.axis_index("expert"), lax.axis_index("mp")
    x, c = dp // 2, lax.rem(dp, 2)
    other = 1 - c
    left, right = lax.rem(x + nx - 1, nx), lax.rem(x + 1, nx)
    far = lax.rem(x + 2, nx)
    y_left, y_right, y_far = lax.rem(y + ny - 1, ny), lax.rem(y + 1, ny), lax.rem(y + 2, ny)
    chunks = wbuf.shape[0]
    part = gate_hbm.shape[1]
    own_rows = part * nz
    chip_rows = 2 * own_rows
    slots = rows.shape[1]
    half = slots // 2
    cap = planes.shape[1]
    feat = tok_out.shape[1]
    lanes = feat // 128
    half_units = chunks * UNITS
    bf16, f32 = jnp.bfloat16, jnp.float32
    partner = (dp - c + other, z, y)

    barrier = pltpu.get_barrier_semaphore()
    peers = [(dp - c + cc, lax.rem(z + o, nz), y) for o in range(1, nz) for cc in (0, 1)]
    peers += [partner, (left * 2 + c, z, y), (right * 2 + c, z, y), (dp, z, y_left), (dp, z, y_right)]
    for peer in peers:
        pl.semaphore_signal(barrier, inc=1, device_id=peer, device_id_type=MESH)

    def stage_copies(k):
        copies = []
        for cc in (0, 1):
            at = pl.multiple_of(cc * half_units + k * UNITS, UNITS)
            copies.append(pltpu.make_async_copy(
                gate_hbm.at[:, :, pl.ds(at, UNITS)], stage.at[k, cc, :, :, pl.ds(0, UNITS)], stage_sem.at[k]))
            copies.append(pltpu.make_async_copy(
                up_hbm.at[:, :, pl.ds(at, UNITS)], stage.at[k, cc, :, :, pl.ds(UNITS, UNITS)], stage_sem.at[k]))
        return copies

    def stage_start(k, _):
        for copy in stage_copies(k):
            copy.start()
        return 0

    lax.fori_loop(0, chunks, stage_start, 0)
    grad_cols = pl.ds(pl.multiple_of(c * half_units, half_units), half_units)
    grad_other = pl.ds(pl.multiple_of(other * half_units, half_units), half_units)
    grad_in = pltpu.make_async_copy(grad_hbm.at[:, grad_cols], grad.at[c], in_sem)
    grad_in.start()
    plane_in = pltpu.make_async_copy(planes_hbm.at[z], planes.at[z], tok_own)
    plane_in.start()

    pl.semaphore_wait(barrier, len(peers))

    my_block = pl.ds(pl.multiple_of(x * chip_rows + c * own_rows + z * part, 16), part)
    offsets = []
    for o in range(1, nz // 2):
        offsets += [o, nz - o]
    offsets.append(nz // 2)

    def send_z(k, _):
        pltpu.make_async_copy(stage.at[k], stage.at[k], stage_sem.at[k]).wait()
        for o in offsets + [0]:
            zt = lax.rem(z + o, nz)
            for cc in ((c, other) if o else (other,)):
                pltpu.make_async_remote_copy(
                    stage.at[k, cc, zt], wbuf.at[k, my_block, :], z_send.at[k], z_recv.at[k],
                    (dp - c + cc, zt, y), MESH).start()
        pltpu.make_async_copy(stage.at[k, c, z], wbuf.at[k, my_block, :], own_sem.at[k]).start()
        return 0

    def plane_out(o):
        zt = lax.rem(z + o, nz)
        return pltpu.make_async_remote_copy(
            planes_hbm.at[zt], planes.at[z], tok_send.at[o - 1], tok_recv.at[z], (dp, zt, y), MESH)

    send_z(0, 0)
    send_z(1, 0)
    for o in offsets:
        plane_out(o).start()
    lax.fori_loop(2, chunks, send_z, 0)

    def to_partner(n, src, dst):
        return pltpu.make_async_remote_copy(src, dst, p_send.at[n], p_recv.at[n], partner, MESH)

    grad_out = to_partner(5, grad_hbm.at[:, grad_other], grad.at[c])
    grad_out.start()

    def rows_of(chip, first, count):
        return pl.ds(pl.multiple_of(chip * chip_rows + first, 16), count)

    def x_copy(k, way, chip, first, count):
        where = wbuf.at[k, rows_of(chip, first, count), :]
        to = right if way % 2 == 0 else left
        return pltpu.make_async_remote_copy(
            where, where, x_send.at[way, k], x_recv.at[way, k], (to * 2 + c, z, y), MESH)

    n_in = 2 * nz - 1

    def step_own(k):
        whole = wbuf.at[k, pl.ds(0, n_in * part), :]
        pltpu.make_async_copy(whole, whole, z_recv.at[k]).wait()
        pltpu.make_async_copy(stage.at[k, c, z], wbuf.at[k, my_block, :], own_sem.at[k]).wait()
        x_copy(k, 0, x, 0, chip_rows).start()
        x_copy(k, 1, x, 0, chip_rows).start()

    def step_relay(k):
        x_copy(k, 0, left, 0, chip_rows).wait_recv()
        x_copy(k, 2, left, 0, own_rows).start()
        x_copy(k, 1, right, 0, chip_rows).wait_recv()
        x_copy(k, 3, right, own_rows, own_rows).start()

    def cols_of(t):
        return pl.ds(pl.multiple_of(t * feat, 128), feat)

    def y_copy(way, t, first, count):
        where = rows.at[c, pl.ds(first, count), cols_of(t)]
        to = y_right if way % 2 == 0 else y_left
        return pltpu.make_async_remote_copy(where, where, y_send.at[way], y_recv.at[way], (dp, z, to), MESH)

    def share(n, t):
        where = rows.at[c, :, cols_of(t)]
        return to_partner(n, where, where)

    def shared(n, t):
        where = rows.at[other, :, cols_of(t)]
        pltpu.make_async_copy(where, where, p_recv.at[n]).wait()

    def gather_rows():
        plane_in.wait()
        for o in offsets:
            zs = lax.rem(z + o, nz)
            pltpu.make_async_copy(planes_hbm.at[zs], planes.at[zs], tok_recv.at[zs]).wait()
        for j in range(nz):
            for n in range(lanes + 1):
                spread[n, pl.ds(j, cap, stride=nz), :] = planes[j, :, n * 128:(n + 1) * 128].astype(f32)
        rows[c, :, cols_of(y)] = jnp.concatenate([spread[n] for n in range(lanes)], axis=1).astype(bf16)
        scale[c] = spread[lanes]
        y_copy(0, y, 0, slots).start()
        y_copy(1, y, 0, slots).start()
        share(0, y).start()
        to_partner(4, scale.at[c], scale.at[c]).start()

    def hid_out(k):
        cols = pl.ds(pl.multiple_of(c * half_units + k * UNITS, UNITS), UNITS)
        here = pltpu.make_async_copy(hid.at[k, c], hid_hbm.at[:, cols], hid_sem.at[k])
        there = pltpu.make_async_remote_copy(
            hid.at[k, other], hid_hbm.at[:, cols], hid_send.at[k], hid_recv.at[k], partner, MESH)
        return here, there

    swaps = (y_far, y_right, y_left, y)

    def swap(n):
        return pltpu.make_async_remote_copy(bsend.at[n], brecv.at[n], b_send.at[n], b_recv.at[n], partner, MESH)

    def compute(k):
        x_copy(k, 2, far, 0, own_rows).wait_recv()
        x_copy(k, 3, far, own_rows, own_rows).wait_recv()
        at = pl.ds(pl.multiple_of(k * UNITS, UNITS), UNITS)
        both = jnp.dot(rows[...].reshape(2 * slots, rows.shape[2]), wbuf[k], preferred_element_type=f32)
        gate, up = both[:, :UNITS], both[:, UNITS:]
        weight = scale[...].reshape(2 * slots, UNITS)
        sig = jax.nn.sigmoid(gate)
        hidden = (weight * gate * sig * up).astype(bf16)
        hid[k] = hidden.reshape(2, slots, UNITS)
        grad_act = weight * grad[:, :, at].reshape(2 * slots, UNITS).astype(f32)
        gate_grad = (grad_act * up * sig * (1.0 + gate * (1.0 - sig))).astype(bf16)
        up_grad = (grad_act * gate * sig).astype(bf16)
        pair = jnp.concatenate([gate_grad, up_grad], axis=1)
        here, there = hid_out(k)
        here.start()
        there.start()
        for n, t in enumerate(swaps):
            cols = cols_of(t)
            term = lax.dot_general(pair, wbuf[k, cols, :], (((1,), (1,)), ((), ())), preferred_element_type=f32)
            term = term.reshape(2, slots, feat)

            @pl.when(k == 0)
            def _():
                acc[:, :, cols] = term

            @pl.when(k > 0)
            def _():
                acc[:, :, cols] = acc[:, :, cols] + term

            @pl.when(k == chunks - 1)
            def _():
                bsend[n] = acc[other, :, cols].astype(bf16)
                swap(n).start()

    step_own(0)
    step_own(1)
    step_relay(0)
    gather_rows()
    step_relay(1)
    y_copy(0, y_left, 0, slots).wait_recv()
    y_copy(2, y_left, 0, half).start()
    share(1, y_left).start()
    y_copy(1, y_right, 0, slots).wait_recv()
    y_copy(3, y_right, half, half).start()
    share(2, y_right).start()
    step_own(2)
    y_copy(2, y_far, 0, half).wait_recv()
    y_copy(3, y_far, half, half).wait_recv()
    share(3, y_far).start()
    grad_in.wait()
    pltpu.make_async_copy(grad_hbm.at[:, grad_other], grad.at[other], p_recv.at[5]).wait()
    pltpu.make_async_copy(scale.at[other], scale.at[other], p_recv.at[4]).wait()
    for n, t in enumerate((y, y_left, y_right, y_far)):
        shared(n, t)

    def main(k, _):
        compute(k)

        @pl.when(k + 3 < chunks)
        def _():
            step_own(k + 3)

        @pl.when(k + 2 < chunks)
        def _():
            step_relay(k + 2)
        return 0

    lax.fori_loop(0, chunks, main, 0)

    upper, lower = pl.ds(0, half), pl.ds(half, half)

    def piece(n):
        to = y_right if n % 2 == 0 else y_left
        return pltpu.make_async_remote_copy(ysend.at[n], yrecv.at[n], ys_send.at[n], ys_recv.at[n], (dp, z, to), MESH)

    def pass_on(n, value):
        ysend[n] = value.astype(bf16)
        piece(n).start()

    swap(0).wait_recv()
    pass_on(0, acc[c, upper, cols_of(y_far)] + brecv[0, upper].astype(f32))
    pass_on(1, acc[c, lower, cols_of(y_far)] + brecv[0, lower].astype(f32))
    swap(1).wait_recv()
    pass_on(2, acc[c, lower, cols_of(y_right)] + brecv[1, lower].astype(f32))
    swap(2).wait_recv()
    pass_on(3, acc[c, upper, cols_of(y_left)] + brecv[2, upper].astype(f32))
    piece(0).wait_recv()
    pass_on(4, acc[c, upper, cols_of(y_right)] + brecv[1, upper].astype(f32) + yrecv[0].astype(f32))
    piece(1).wait_recv()
    pass_on(5, acc[c, lower, cols_of(y_left)] + brecv[2, lower].astype(f32) + yrecv[1].astype(f32))
    swap(3).wait_recv()

    def give_back(h, o):
        zt = lax.rem(z + o, nz)
        return pltpu.make_async_remote_copy(
            zsend.at[h, zt], back.at[h, z], r_send.at[h, o - 1], r_recv.at[h, z], (dp, zt, y), MESH)

    def keep(h):
        return pltpu.make_async_copy(zsend.at[h, z], back.at[h, z], r_own.at[h])

    for h, (near, via) in enumerate(((3, 4), (2, 5))):
        which = (upper, lower)[h]
        piece(near).wait_recv()
        piece(via).wait_recv()
        total = (acc[c, which, cols_of(y)] + brecv[3, which].astype(f32)
                 + yrecv[near].astype(f32) + yrecv[via].astype(f32))
        for n in range(lanes):
            final[n] = total[:, n * 128:(n + 1) * 128]
        for j in range(nz):
            zsend[h, j] = jnp.concatenate(
                [final[n, pl.ds(j, cap // 2, stride=nz), :] for n in range(lanes)], axis=1).astype(bf16)
        for o in offsets:
            give_back(h, o).start()
        keep(h).start()

    def drain(k, _):
        whole = wbuf.at[k, pl.ds(0, n_in * part), :]
        pltpu.make_async_copy(whole, whole, z_send.at[k]).wait()
        x_copy(k, 0, x, 0, chip_rows).wait_send()
        x_copy(k, 1, x, 0, chip_rows).wait_send()
        x_copy(k, 2, left, 0, own_rows).wait_send()
        x_copy(k, 3, right, own_rows, own_rows).wait_send()
        here, there = hid_out(k)
        here.wait()
        there.wait_send()
        cols = pl.ds(pl.multiple_of(other * half_units + k * UNITS, UNITS), UNITS)
        pltpu.make_async_copy(hid.at[k, other], hid_hbm.at[:, cols], hid_recv.at[k]).wait()
        return 0

    lax.fori_loop(0, chunks, drain, 0)
    for o in offsets:
        plane_out(o).wait_send()
    y_copy(0, y, 0, slots).wait_send()
    y_copy(1, y, 0, slots).wait_send()
    y_copy(2, y_left, 0, half).wait_send()
    y_copy(3, y_right, half, half).wait_send()
    for n, t in enumerate((y, y_left, y_right, y_far)):
        share(n, t).wait_send()
    to_partner(4, scale.at[c], scale.at[c]).wait_send()
    grad_out.wait_send()
    for n in range(4):
        swap(n).wait_send()
    for n in range(6):
        piece(n).wait_send()

    for h in (0, 1):
        keep(h).wait()
        for o in offsets:
            zs = lax.rem(z + o, nz)
            pltpu.make_async_copy(zsend.at[h, zs], back.at[h, zs], r_recv.at[h, zs]).wait()
            give_back(h, o).wait_send()
        for e in range(nz):
            for n in range(lanes):
                spread[n, pl.ds(h * half + e, cap // 2, stride=nz), :] = back[h, e, :, n * 128:(n + 1) * 128].astype(f32)
    gathered = jnp.concatenate([spread[n] for n in range(lanes)], axis=1).astype(bf16)
    tok_out[...] = jnp.dot(select[...], gathered, preferred_element_type=f32).astype(bf16)


def stream(nx, nz, ny, select, planes, w_gate, w_up, grad):
    slots, hidden = grad.shape
    cap = planes.shape[1]
    feat = planes.shape[2] - 128
    d = feat * ny
    tokens = select.shape[0]
    chunks = hidden // 2 // UNITS
    part = w_gate.shape[1]
    bf16, f32 = jnp.bfloat16, jnp.float32
    dma = pltpu.SemaphoreType.DMA
    return pl.pallas_call(
        functools.partial(stream_kernel, nx, nz, ny),
        out_shape=(jax.ShapeDtypeStruct((slots, hidden), bf16), jax.ShapeDtypeStruct((tokens, feat), bf16)),
        in_specs=[pl.BlockSpec(memory_space=pltpu.VMEM)] + [pl.BlockSpec(memory_space=pl.ANY)] * 4,
        out_specs=(pl.BlockSpec(memory_space=pl.ANY), pl.BlockSpec(memory_space=pltpu.VMEM)),
        scratch_shapes=[
            pltpu.VMEM((chunks, 2, nz, part, 2 * UNITS), bf16),
            pltpu.VMEM((chunks, d, 2 * UNITS), bf16),
            pltpu.VMEM((nz, cap, feat + 128), bf16),
            pltpu.VMEM((feat // 128 + 1, slots, 128), f32),
            pltpu.VMEM((2, slots, d), bf16),
            pltpu.VMEM((2, slots, UNITS), f32),
            pltpu.VMEM((2, slots, hidden // 2), bf16),
            pltpu.VMEM((chunks, 2, slots, UNITS), bf16),
            pltpu.VMEM((2, slots, d), f32),
            pltpu.VMEM((4, slots, feat), bf16),
            pltpu.VMEM((4, slots, feat), bf16),
            pltpu.VMEM((6, slots // 2, feat), bf16),
            pltpu.VMEM((6, slots // 2, feat), bf16),
            pltpu.VMEM((feat // 128, slots // 2, 128), f32),
            pltpu.VMEM((2, nz, cap // 2, feat), bf16),
            pltpu.VMEM((2, nz, cap // 2, feat), bf16),
            dma((chunks,)), dma((chunks,)), dma((chunks,)), dma((chunks,)), dma((4, chunks)), dma((4, chunks)),
            dma(()), dma((nz - 1,)), dma((nz,)), dma((4,)), dma((4,)),
            dma(()), dma((6,)), dma((6,)), dma((chunks,)), dma((chunks,)), dma((chunks,)),
            dma((4,)), dma((4,)), dma((6,)), dma((6,)),
            dma((2,)), dma((2, nz - 1)), dma((2, nz)),
        ],
        compiler_params=pltpu.CompilerParams(
            collective_id=0, has_side_effects=True, vmem_limit_bytes=62 * 1024 * 1024),
        name="stream",
    )(select, planes, w_gate, w_up, grad)


def per_device(nx, nz, ny, tokens, expert_ids, route_weight, w_gate, w_up, grad_hidden):
    slots_cap = grad_hidden.shape[3]
    feat = tokens.shape[1]
    hidden_part = w_gate.shape[2]
    slots = nz * slots_cap
    placed = slot_map(expert_ids, nz, slots_cap).astype(jnp.float32)
    select = jnp.sum(placed, axis=1)
    by_expert = select.reshape(-1, slots_cap, nz).transpose(2, 1, 0).reshape(slots, -1)
    sent_rows = jnp.dot(by_expert.astype(jnp.bfloat16), tokens, preferred_element_type=jnp.float32).astype(jnp.bfloat16)
    sent_scale = jnp.einsum("tks,tk->s", placed, route_weight.astype(jnp.float32),
                            precision=lax.Precision.HIGHEST).astype(jnp.bfloat16)
    sent_scale = sent_scale.reshape(slots_cap, nz).T.reshape(slots)
    planes = jnp.concatenate([sent_rows, jnp.broadcast_to(sent_scale[:, None], (slots, 128))], axis=1)
    planes = planes.reshape(nz, slots_cap, feat + 128)
    grad = grad_hidden.transpose(0, 1, 3, 2, 4).reshape(slots, hidden_part)
    hidden, grad_tokens = stream(nx, nz, ny, select.astype(jnp.bfloat16), planes, w_gate, w_up, grad)
    hidden_out = hidden.reshape(1, 1, slots_cap, nz, hidden_part).transpose(0, 1, 3, 2, 4)
    return hidden_out, grad_tokens


def solution(mesh):
    nx, nz, ny = mesh.shape["dp"] // 2, mesh.shape["expert"], mesh.shape["mp"]
    in_specs = (
        P(("dp", "expert"), "mp"),
        P(("dp", "expert"), None),
        P(("dp", "expert"), None),
        P(None, ("dp", "expert"), "mp"),
        P(None, ("dp", "expert"), "mp"),
        P("expert", "dp", None, None, "mp"),
    )
    out_specs = (P("expert", "dp", None, None, "mp"), P(("dp", "expert"), "mp"))
    return jax.shard_map(
        functools.partial(per_device, nx, nz, ny), mesh=mesh, in_specs=in_specs, out_specs=out_specs, check_vma=False
    )
```

time: 260 us -> 190 us (0.73)
  waiting for transfers between devices: 73.3 us -> 0 us
  Pallas kernels: 130 us -> 180 us
  blocking collectives: 25.9 us -> 0 us
  between operations: 14.2 us -> 0.75 us
  starting transfers between devices: 6.82 us -> 0 us
    pallas_call x1, Pallas kernels: 130 us -> 180 us  [stream(): pl.pallas_call(functools.partial(stream_kernel, nx, nz, ny), out_shape=(j...]
    all_gather x1 -> x0, waiting for transfers between devices: 28 us -> none  [per_device(): rows_full = lax.all_gather(both[:, :feat], 'mp', axis=1, tiled=True)]
    reduce_scatter x1 -> x0, waiting for transfers between devices: 28 us -> none  [per_device(): shared = lax.psum_scatter(back, 'mp', scatter_dimension=1, tiled=True)]
    all_to_all x1 -> x0, blocking collectives: 25.9 us -> none  [per_device(): lax.all_to_all(both, 'expert', split_axis=0, concat_axis=0, tiled=True)]
    all_to_all x1 -> x0, waiting for transfers between devices: 17.2 us -> none  [per_device(): lax.all_to_all(shared, 'expert', split_axis=0, concat_axis=0, tiled=True)]
    all_to_all x1 -> x0, starting transfers between devices: 6.74 us -> none  [per_device(): lax.all_to_all(shared, 'expert', split_axis=0, concat_axis=0, tiled=True)]
  transfers between devices with their start and end apart: 3 -> 0, of which waited for: 3 -> 0; matrix products, arithmetic and copies ran while one was open for 0% -> 0% of each run, Pallas kernels for 0% -> 0%
where the time goes in v2:
time: 190 us
  Pallas kernels  180 us (95%)
  local copies, waits for them, and re-layouts  6.72 us (4%)
    pallas_call x1, Pallas kernels, stream(): pl.pallas_call(functools.partial(stream_kernel, nx, nz, ny), out_shape=(j...  180 us
    unnamed x7, local copies, waits for them, and re-layouts  3.97 us

profile of v2, /device:TPU:1, one launch (start us, length us, event | category | flops | bytes accessed | tf_op | source)
XLA Modules:
  0.0 189.9 jit_solution(2350719475838232650)
XLA Ops:
  0.6 0.0 copy-start
  0.6 0.8 copy.23
  1.5 0.1 eq.43
  1.6 0.1 eq.39
  1.8 0.6 reduce-window.6
  2.4 0.2 slice_reduce_fusion
  2.6 0.1 fusion.2
  2.7 0.1 mul.19
  2.9 0.1 copy.25
  2.9 0.7 add.7
  3.6 0.8 convolution_reduce_fusion
  4.5 0.1 reshape.59
  4.6 0.1 copy.27
  4.7 0.1 broadcast_in_dim.4
  4.7 0.1 convert_reduce_fusion
  4.8 0.1 broadcast_in_dim.5
  5.0 0.8 copy.28.select
  5.7 0.0 copy-done
  5.7 0.3 convolution_convert_fusion
  6.0 0.9 reshape.60.planes_hbm
  7.0 179.8 %stream.1 = (bf16[288,2048]{1,0:T(8,128)(2,1)}, bf16[128,768]{1,0:T(8,128)(2,1)}) custom-call(bf16[128,288]{1,0:T(8,128)(2,1)} %copy.28.select, bf16[8,36,896]{2,1,0:T(8,128)(2,1)} %reshape.60.planes_hbm, bf16[8,48,2048]{2,1,0:T(8,128)(2,1)} %gate_hbm.1, bf16[8,48,2048]{2,1,0:T(8,128)(2,1)} %up_hbm.1, bf16[288,2048]{1,0:T(8,128)(2,1)} %bitcast.21), custom_call_target="tpu_custom_call" | custom-call | tf_op jit(solution)/shard_map/stream/pallas_call | solution.py:349
  186.8 0.0 copy-start.1
  186.8 2.4 %copy.34 = bf16[1,1,8,36,2048]{4,2,3,1,0:T(8,128)(2,1)} copy(bf16[1,1,8,36,2048]{4,2,3,1,0:T(8,128)(2,1)} %bitcast.22) | data formatting | bytes 2359296
  189.2 0.0 copy-done.1
  189.2 0.7 copy.35
  (7 shorter events, 0.1 us)
Async XLA Ops:
  0.6 5.1 %copy-start = (bf16[128,768]{1,0:T(8,128)(2,1)S(1)}, bf16[128,768]{1,0:T(8,128)(2,1)}, u32[]{:S(2)}) copy-start(bf16[128,768]{1,0:T(8,128)(2,1)} %param.6) | copy-start | bytes 589828
  186.8 2.5 %copy-start.1 = (bf16[128,768]{1,0:T(8,128)(2,1)S(1)}, bf16[128,768]{1,0:T(8,128)(2,1)}, u32[]{:S(2)}) copy-start(bf16[128,768]{1,0:T(8,128)(2,1)} %get-tuple-element.9) | copy-start | bytes 589828

commit v3 on v2

--- a/solution.py
+++ b/solution.py
@@ -21,8 +21,8 @@
     return placed.reshape(expert_ids.shape[0], expert_ids.shape[1], n_expert * slots_cap)
 
 
-def stream_kernel(nx, nz, ny, select, planes_hbm, gate_hbm, up_hbm, grad_hbm, hid_hbm, tok_out,
-                  stage, wbuf, planes, spread, rows, scale, grad, hid, acc, bsend, brecv, ysend, yrecv, final, zsend, back,
+def stream_kernel(nx, nz, ny, pairs_of, select, planes_hbm, gate_hbm, up_hbm, grad_hbm, hid_hbm, tok_out,
+                  stage, wbuf, pairs, planes, spread, rows, scale, grad, hid, acc, bsend, brecv, ysend, yrecv, final, zsend, back,
                   stage_sem, own_sem, z_send, z_recv, x_send, x_recv, tok_own, tok_send, tok_recv, y_send, y_recv,
                   in_sem, p_send, p_recv, hid_sem, hid_send, hid_recv, b_send, b_recv, ys_send, ys_recv,
                   r_own, r_send, r_recv):
@@ -77,10 +77,11 @@
     pl.semaphore_wait(barrier, len(peers))
 
     my_block = pl.ds(pl.multiple_of(x * chip_rows + c * own_rows + z * part, 16), part)
-    offsets = []
-    for o in range(1, nz // 2):
+    across = nz // 2
+    early = 4
+    offsets = [across]
+    for o in range(across - 1, 0, -1):
         offsets += [o, nz - o]
-    offsets.append(nz // 2)
 
     def send_z(k, _):
         pltpu.make_async_copy(stage.at[k], stage.at[k], stage_sem.at[k]).wait()
@@ -98,11 +99,21 @@
         return pltpu.make_async_remote_copy(
             planes_hbm.at[zt], planes.at[z], tok_send.at[o - 1], tok_recv.at[z], (dp, zt, y), MESH)
 
-    send_z(0, 0)
-    send_z(1, 0)
+    pltpu.make_async_copy(stage.at[0], stage.at[0], stage_sem.at[0]).wait()
+    pltpu.make_async_copy(stage.at[0, c, z], wbuf.at[0, my_block, :], own_sem.at[0]).start()
+    for part_of in (0, 1):
+        lane = pl.ds(part_of * UNITS, UNITS)
+        slot = part_of * chunks
+        for o in offsets + [0]:
+            zt = lax.rem(z + o, nz)
+            for cc in ((c, other) if o else (other,)):
+                pltpu.make_async_remote_copy(
+                    stage.at[0, cc, zt, :, lane], wbuf.at[0, my_block, lane], z_send.at[slot], z_recv.at[slot],
+                    (dp - c + cc, zt, y), MESH).start()
+    lax.fori_loop(1, early, send_z, 0)
     for o in offsets:
         plane_out(o).start()
-    lax.fori_loop(2, chunks, send_z, 0)
+    lax.fori_loop(early, chunks, send_z, 0)
 
     def to_partner(n, src, dst):
         return pltpu.make_async_remote_copy(src, dst, p_send.at[n], p_recv.at[n], partner, MESH)
@@ -113,11 +124,13 @@
     def rows_of(chip, first, count):
         return pl.ds(pl.multiple_of(chip * chip_rows + first, 16), count)
 
-    def x_copy(k, way, chip, first, count):
-        where = wbuf.at[k, rows_of(chip, first, count), :]
+    def x_copy(k, way, chip, first, count, part_of=None):
+        lane = pl.ds(0, 2 * UNITS) if part_of is None else pl.ds(part_of * UNITS, UNITS)
+        slot = chunks if part_of == 1 else k
+        where = wbuf.at[k, rows_of(chip, first, count), lane]
         to = right if way % 2 == 0 else left
         return pltpu.make_async_remote_copy(
-            where, where, x_send.at[way, k], x_recv.at[way, k], (to * 2 + c, z, y), MESH)
+            where, where, x_send.at[way, slot], x_recv.at[way, slot], (to * 2 + c, z, y), MESH)
 
     n_in = 2 * nz - 1
 
@@ -128,11 +141,17 @@
         x_copy(k, 0, x, 0, chip_rows).start()
         x_copy(k, 1, x, 0, chip_rows).start()
 
-    def step_relay(k):
-        x_copy(k, 0, left, 0, chip_rows).wait_recv()
-        x_copy(k, 2, left, 0, own_rows).start()
-        x_copy(k, 1, right, 0, chip_rows).wait_recv()
-        x_copy(k, 3, right, own_rows, own_rows).start()
+    def step_relay(k, part_of=None):
+        x_copy(k, 0, left, 0, chip_rows, part_of).wait_recv()
+        x_copy(k, 2, left, 0, own_rows, part_of).start()
+        x_copy(k, 1, right, 0, chip_rows, part_of).wait_recv()
+        x_copy(k, 3, right, own_rows, own_rows, part_of).start()
+
+    def first_own(part_of):
+        whole = wbuf.at[0, pl.ds(0, n_in * part), pl.ds(part_of * UNITS, UNITS)]
+        pltpu.make_async_copy(whole, whole, z_recv.at[part_of * chunks]).wait()
+        x_copy(0, 0, x, 0, chip_rows, part_of).start()
+        x_copy(0, 1, x, 0, chip_rows, part_of).start()
 
     def cols_of(t):
         return pl.ds(pl.multiple_of(t * feat, 128), feat)
@@ -178,8 +197,10 @@
         return pltpu.make_async_remote_copy(bsend.at[n], brecv.at[n], b_send.at[n], b_recv.at[n], partner, MESH)
 
     def compute(k):
-        x_copy(k, 2, far, 0, own_rows).wait_recv()
-        x_copy(k, 3, far, own_rows, own_rows).wait_recv()
+        @pl.when(k > 0)
+        def _():
+            x_copy(k, 2, far, 0, own_rows).wait_recv()
+            x_copy(k, 3, far, own_rows, own_rows).wait_recv()
         at = pl.ds(pl.multiple_of(k * UNITS, UNITS), UNITS)
         both = jnp.dot(rows[...].reshape(2 * slots, rows.shape[2]), wbuf[k], preferred_element_type=f32)
         gate, up = both[:, :UNITS], both[:, UNITS:]
@@ -190,40 +211,46 @@
         grad_act = weight * grad[:, :, at].reshape(2 * slots, UNITS).astype(f32)
         gate_grad = (grad_act * up * sig * (1.0 + gate * (1.0 - sig))).astype(bf16)
         up_grad = (grad_act * gate * sig).astype(bf16)
-        pair = jnp.concatenate([gate_grad, up_grad], axis=1)
+        pairs[:, :UNITS] = gate_grad
+        pairs[:, UNITS:] = up_grad
         here, there = hid_out(k)
         here.start()
         there.start()
-        for n, t in enumerate(swaps):
-            cols = cols_of(t)
-            term = lax.dot_general(pair, wbuf[k, cols, :], (((1,), (1,)), ((), ())), preferred_element_type=f32)
-            term = term.reshape(2, slots, feat)
-
-            @pl.when(k == 0)
-            def _():
-                acc[:, :, cols] = term
-
-            @pl.when(k > 0)
-            def _():
-                acc[:, :, cols] = acc[:, :, cols] + term
+
+        def backward(n, _):
+            cols = cols_of(lax.rem(y + 2 + 3 * n + 3 * (n // 2) + 2 * (n // 3), ny))
+            term = lax.dot_general(pairs[...], wbuf[k, cols, :], (((1,), (1,)), ((), ())), preferred_element_type=f32)
+            acc[:, :, cols] += term.reshape(2, slots, feat)
 
             @pl.when(k == chunks - 1)
             def _():
                 bsend[n] = acc[other, :, cols].astype(bf16)
                 swap(n).start()
-
-    step_own(0)
+            return 0
+
+        lax.fori_loop(0, ny, backward, 0)
+
+    acc[...] = jnp.zeros_like(acc)
+    pltpu.make_async_copy(stage.at[0, c, z], wbuf.at[0, my_block, :], own_sem.at[0]).wait()
+    first_own(0)
+    first_own(1)
+    step_relay(0, 0)
+    step_relay(0, 1)
     step_own(1)
-    step_relay(0)
+    step_own(2)
+    step_relay(1)
+    step_own(3)
+    step_relay(2)
     gather_rows()
-    step_relay(1)
+    step_relay(3)
+    step_own(4)
     y_copy(0, y_left, 0, slots).wait_recv()
     y_copy(2, y_left, 0, half).start()
     share(1, y_left).start()
     y_copy(1, y_right, 0, slots).wait_recv()
     y_copy(3, y_right, half, half).start()
     share(2, y_right).start()
-    step_own(2)
+    step_own(5)
     y_copy(2, y_far, 0, half).wait_recv()
     y_copy(3, y_far, half, half).wait_recv()
     share(3, y_far).start()
@@ -233,73 +260,108 @@
     for n, t in enumerate((y, y_left, y_right, y_far)):
         shared(n, t)
 
+    for part_of in (0, 1):
+        x_copy(0, 2, far, 0, own_rows, part_of).wait_recv()
+        x_copy(0, 3, far, own_rows, own_rows, part_of).wait_recv()
+
     def main(k, _):
         compute(k)
 
-        @pl.when(k + 3 < chunks)
-        def _():
-            step_own(k + 3)
-
-        @pl.when(k + 2 < chunks)
-        def _():
-            step_relay(k + 2)
+        @pl.when(k == 0)
+        def _():
+            step_relay(4)
+            step_own(6)
+
+        @pl.when(k == 2)
+        def _():
+            step_relay(5)
+            step_own(7)
+
+        @pl.when(k == 4)
+        def _():
+            step_relay(6)
+
+        @pl.when(k == 5)
+        def _():
+            step_relay(7)
         return 0
 
     lax.fori_loop(0, chunks, main, 0)
 
-    upper, lower = pl.ds(0, half), pl.ds(half, half)
-
-    def piece(n):
-        to = y_right if n % 2 == 0 else y_left
-        return pltpu.make_async_remote_copy(ysend.at[n], yrecv.at[n], ys_send.at[n], ys_recv.at[n], (dp, z, to), MESH)
-
-    def pass_on(n, value):
-        ysend[n] = value.astype(bf16)
-        piece(n).start()
+    subs = 2 * pairs_of
+    sub = slots // subs
+    per = cap // pairs_of
+
+    def piece(kind, n):
+        to = y_right if (n + kind) % 2 == 0 else y_left
+        at = (kind // 2) * subs + n if kind % 2 == 0 else 2 * subs + n
+        return pltpu.make_async_remote_copy(
+            ysend.at[at], yrecv.at[at], ys_send.at[at], ys_recv.at[at], (dp, z, to), MESH)
+
+    def got(kind, n):
+        at = (kind // 2) * subs + n if kind % 2 == 0 else 2 * subs + n
+        piece(kind, n).wait_recv()
+        return yrecv[at].astype(f32)
+
+    def pass_on(kind, n, value):
+        at = (kind // 2) * subs + n if kind % 2 == 0 else 2 * subs + n
+        ysend[at] = value.astype(bf16)
+        piece(kind, n).start()
+
+    def mine(order, n):
+        rows_n = pl.ds(n * sub, sub)
+        return acc[c, rows_n, cols_of(swaps[order])] + brecv[order, rows_n].astype(f32)
 
     swap(0).wait_recv()
-    pass_on(0, acc[c, upper, cols_of(y_far)] + brecv[0, upper].astype(f32))
-    pass_on(1, acc[c, lower, cols_of(y_far)] + brecv[0, lower].astype(f32))
+    for n in range(subs):
+        pass_on(0, n, mine(0, n))
     swap(1).wait_recv()
-    pass_on(2, acc[c, lower, cols_of(y_right)] + brecv[1, lower].astype(f32))
     swap(2).wait_recv()
-    pass_on(3, acc[c, upper, cols_of(y_left)] + brecv[2, upper].astype(f32))
-    piece(0).wait_recv()
-    pass_on(4, acc[c, upper, cols_of(y_right)] + brecv[1, upper].astype(f32) + yrecv[0].astype(f32))
-    piece(1).wait_recv()
-    pass_on(5, acc[c, lower, cols_of(y_left)] + brecv[2, lower].astype(f32) + yrecv[1].astype(f32))
+    for g in range(pairs_of):
+        for n in (2 * g + 1, 2 * g):
+            pass_on(1, n, mine(1 if n % 2 else 2, n))
+        for n in (2 * g, 2 * g + 1):
+            pass_on(2, n, mine(2 if n % 2 else 1, n) + got(0, n))
     swap(3).wait_recv()
 
-    def give_back(h, o):
+    def give_back(g, o):
         zt = lax.rem(z + o, nz)
         return pltpu.make_async_remote_copy(
-            zsend.at[h, zt], back.at[h, z], r_send.at[h, o - 1], r_recv.at[h, z], (dp, zt, y), MESH)
-
-    def keep(h):
-        return pltpu.make_async_copy(zsend.at[h, z], back.at[h, z], r_own.at[h])
-
-    for h, (near, via) in enumerate(((3, 4), (2, 5))):
-        which = (upper, lower)[h]
-        piece(near).wait_recv()
-        piece(via).wait_recv()
-        total = (acc[c, which, cols_of(y)] + brecv[3, which].astype(f32)
-                 + yrecv[near].astype(f32) + yrecv[via].astype(f32))
-        for n in range(lanes):
-            final[n] = total[:, n * 128:(n + 1) * 128]
+            zsend.at[g, zt], back.at[g, z], r_send.at[g, o - 1], r_recv.at[g, z], (dp, zt, y), MESH)
+
+    def keep(g):
+        return pltpu.make_async_copy(zsend.at[g, z], back.at[g, z], r_own.at[g])
+
+    for g in range(pairs_of):
+        for i in (0, 1):
+            n = 2 * g + i
+            total = mine(3, n) + got(1, n) + got(2, n)
+            for m in range(lanes):
+                final[m, pl.ds(i * sub, sub), :] = total[:, m * 128:(m + 1) * 128]
         for j in range(nz):
-            zsend[h, j] = jnp.concatenate(
-                [final[n, pl.ds(j, cap // 2, stride=nz), :] for n in range(lanes)], axis=1).astype(bf16)
+            zsend[g, j] = jnp.concatenate(
+                [final[m, pl.ds(j, per, stride=nz), :] for m in range(lanes)], axis=1).astype(bf16)
         for o in offsets:
-            give_back(h, o).start()
-        keep(h).start()
+            give_back(g, o).start()
+        keep(g).start()
+
+    def sent(k, part_of):
+        x_copy(k, 0, x, 0, chip_rows, part_of).wait_send()
+        x_copy(k, 1, x, 0, chip_rows, part_of).wait_send()
+        x_copy(k, 2, left, 0, own_rows, part_of).wait_send()
+        x_copy(k, 3, right, own_rows, own_rows, part_of).wait_send()
+
+    for part_of in (0, 1):
+        whole = wbuf.at[0, pl.ds(0, n_in * part), pl.ds(part_of * UNITS, UNITS)]
+        pltpu.make_async_copy(whole, whole, z_send.at[part_of * chunks]).wait()
+        sent(0, part_of)
 
     def drain(k, _):
-        whole = wbuf.at[k, pl.ds(0, n_in * part), :]
-        pltpu.make_async_copy(whole, whole, z_send.at[k]).wait()
-        x_copy(k, 0, x, 0, chip_rows).wait_send()
-        x_copy(k, 1, x, 0, chip_rows).wait_send()
-        x_copy(k, 2, left, 0, own_rows).wait_send()
-        x_copy(k, 3, right, own_rows, own_rows).wait_send()
+        @pl.when(k > 0)
+        def _():
+            whole = wbuf.at[k, pl.ds(0, n_in * part), :]
+            pltpu.make_async_copy(whole, whole, z_send.at[k]).wait()
+            sent(k, None)
         here, there = hid_out(k)
         here.wait()
         there.wait_send()
@@ -320,20 +382,26 @@
     grad_out.wait_send()
     for n in range(4):
         swap(n).wait_send()
-    for n in range(6):
-        piece(n).wait_send()
-
-    for h in (0, 1):
-        keep(h).wait()
+    for kind in range(3):
+        for n in range(subs):
+            piece(kind, n).wait_send()
+
+    result = jnp.zeros(tok_out.shape, f32)
+    for g in range(pairs_of):
+        keep(g).wait()
         for o in offsets:
             zs = lax.rem(z + o, nz)
-            pltpu.make_async_copy(zsend.at[h, zs], back.at[h, zs], r_recv.at[h, zs]).wait()
-            give_back(h, o).wait_send()
+            pltpu.make_async_copy(zsend.at[g, zs], back.at[g, zs], r_recv.at[g, zs]).wait()
         for e in range(nz):
-            for n in range(lanes):
-                spread[n, pl.ds(h * half + e, cap // 2, stride=nz), :] = back[h, e, :, n * 128:(n + 1) * 128].astype(f32)
-    gathered = jnp.concatenate([spread[n] for n in range(lanes)], axis=1).astype(bf16)
-    tok_out[...] = jnp.dot(select[...], gathered, preferred_element_type=f32).astype(bf16)
+            for m in range(lanes):
+                spread[m, pl.ds(2 * g * sub + e, per, stride=nz), :] = back[g, e, :, m * 128:(m + 1) * 128].astype(f32)
+        rows_g = pl.ds(2 * g * sub, 2 * sub)
+        gathered = jnp.concatenate([spread[m, rows_g, :] for m in range(lanes)], axis=1).astype(bf16)
+        result += lax.dot_general(select[rows_g, :], gathered, (((0,), (0,)), ((), ())), preferred_element_type=f32)
+    for g in range(pairs_of):
+        for o in offsets:
+            give_back(g, o).wait_send()
+    tok_out[...] = result.astype(bf16)
 
 
 def stream(nx, nz, ny, select, planes, w_gate, w_up, grad):
@@ -341,19 +409,21 @@
     cap = planes.shape[1]
     feat = planes.shape[2] - 128
     d = feat * ny
-    tokens = select.shape[0]
+    tokens = select.shape[1]
+    pairs_of = 3
     chunks = hidden // 2 // UNITS
     part = w_gate.shape[1]
     bf16, f32 = jnp.bfloat16, jnp.float32
     dma = pltpu.SemaphoreType.DMA
     return pl.pallas_call(
-        functools.partial(stream_kernel, nx, nz, ny),
+        functools.partial(stream_kernel, nx, nz, ny, pairs_of),
         out_shape=(jax.ShapeDtypeStruct((slots, hidden), bf16), jax.ShapeDtypeStruct((tokens, feat), bf16)),
         in_specs=[pl.BlockSpec(memory_space=pltpu.VMEM)] + [pl.BlockSpec(memory_space=pl.ANY)] * 4,
         out_specs=(pl.BlockSpec(memory_space=pl.ANY), pl.BlockSpec(memory_space=pltpu.VMEM)),
         scratch_shapes=[
             pltpu.VMEM((chunks, 2, nz, part, 2 * UNITS), bf16),
             pltpu.VMEM((chunks, d, 2 * UNITS), bf16),
+            pltpu.VMEM((2 * slots, 2 * UNITS), bf16),
             pltpu.VMEM((nz, cap, feat + 128), bf16),
             pltpu.VMEM((feat // 128 + 1, slots, 128), f32),
             pltpu.VMEM((2, slots, d), bf16),
@@ -363,16 +433,17 @@
             pltpu.VMEM((2, slots, d), f32),
             pltpu.VMEM((4, slots, feat), bf16),
             pltpu.VMEM((4, slots, feat), bf16),
-            pltpu.VMEM((6, slots // 2, feat), bf16),
-            pltpu.VMEM((6, slots // 2, feat), bf16),
-            pltpu.VMEM((feat // 128, slots // 2, 128), f32),
-            pltpu.VMEM((2, nz, cap // 2, feat), bf16),
-            pltpu.VMEM((2, nz, cap // 2, feat), bf16),
-            dma((chunks,)), dma((chunks,)), dma((chunks,)), dma((chunks,)), dma((4, chunks)), dma((4, chunks)),
+            pltpu.VMEM((6 * pairs_of, slots // (2 * pairs_of), feat), bf16),
+            pltpu.VMEM((6 * pairs_of, slots // (2 * pairs_of), feat), bf16),
+            pltpu.VMEM((feat // 128, slots // pairs_of, 128), f32),
+            pltpu.VMEM((pairs_of, nz, cap // pairs_of, feat), bf16),
+            pltpu.VMEM((pairs_of, nz, cap // pairs_of, feat), bf16),
+            dma((chunks,)), dma((chunks,)), dma((chunks + 1,)), dma((chunks + 1,)),
+            dma((4, chunks + 1)), dma((4, chunks + 1)),
             dma(()), dma((nz - 1,)), dma((nz,)), dma((4,)), dma((4,)),
             dma(()), dma((6,)), dma((6,)), dma((chunks,)), dma((chunks,)), dma((chunks,)),
-            dma((4,)), dma((4,)), dma((6,)), dma((6,)),
-            dma((2,)), dma((2, nz - 1)), dma((2, nz)),
+            dma((4,)), dma((4,)), dma((6 * pairs_of,)), dma((6 * pairs_of,)),
+            dma((pairs_of,)), dma((pairs_of, nz - 1)), dma((pairs_of, nz)),
         ],
         compiler_params=pltpu.CompilerParams(
             collective_id=0, has_side_effects=True, vmem_limit_bytes=62 * 1024 * 1024),
@@ -395,7 +466,7 @@
     planes = jnp.concatenate([sent_rows, jnp.broadcast_to(sent_scale[:, None], (slots, 128))], axis=1)
     planes = planes.reshape(nz, slots_cap, feat + 128)
     grad = grad_hidden.transpose(0, 1, 3, 2, 4).reshape(slots, hidden_part)
-    hidden, grad_tokens = stream(nx, nz, ny, select.astype(jnp.bfloat16), planes, w_gate, w_up, grad)
+    hidden, grad_tokens = stream(nx, nz, ny, select.T.astype(jnp.bfloat16), planes, w_gate, w_up, grad)
     hidden_out = hidden.reshape(1, 1, slots_cap, nz, hidden_part).transpose(0, 1, 3, 2, 4)
     return hidden_out, grad_tokens
 

time: 190 us -> 164 us (0.86)
  Pallas kernels: 180 us -> 155 us
    pallas_call x1, Pallas kernels: 180 us -> 155 us  [stream(): pl.pallas_call(functools.partial(stream_kernel, nx, nz, ny, pairs_of), ou...]
    unnamed x7 -> x9, local copies, waits for them, and re-layouts: 3.97 us -> 3.97 us
where the time goes in v3:
time: 164 us
  Pallas kernels  155 us (95%)
  local copies, waits for them, and re-layouts  5.97 us (4%)
    pallas_call x1, Pallas kernels, stream(): pl.pallas_call(functools.partial(stream_kernel, nx, nz, ny, pairs_of), ou...  155 us
    unnamed x9, local copies, waits for them, and re-layouts  3.97 us

profile of v3, /device:TPU:1, one launch (start us, length us, event | category | flops | bytes accessed | tf_op | source)
XLA Modules:
  0.0 164.0 jit_solution(1124884864817459537)
XLA Ops:
  0.6 0.0 copy-start
  0.6 0.8 copy.20
  1.5 0.1 eq.43
  1.6 0.1 eq.39
  1.8 0.6 reduce-window.6
  2.4 0.2 slice_reduce_fusion
  2.6 0.1 fusion.2
  2.7 0.1 mul.19
  2.9 0.1 copy.22
  2.9 0.7 add.7
  3.6 0.8 convolution_reduce_fusion
  4.5 0.1 reshape.59
  4.6 0.1 copy.24
  4.7 0.1 broadcast_in_dim.4
  4.7 0.1 convert_reduce_fusion
  4.8 0.0 copy-start.1
  4.8 0.1 broadcast_in_dim.5
  5.0 0.0 copy-done
  5.0 0.3 convolution_convert_fusion
  5.3 0.9 reshape.60.planes_hbm
  6.2 0.0 copy-done.1
  6.2 154.7 %stream.1 = (bf16[288,2048]{1,0:T(8,128)(2,1)}, bf16[128,768]{1,0:T(8,128)(2,1)}) custom-call(bf16[288,128]{1,0:T(8,128)(2,1)} %bitcast.30, bf16[8,36,896]{2,1,0:T(8,128)(2,1)} %reshape.60.planes_hbm, bf16[8,48,2048]{2,1,0:T(8,128)(2,1)} %gate_hbm.1, bf16[8,48,2048]{2,1,0:T(8,128)(2,1)} %up_hbm.1, bf16[288,2048]{1,0:T(8,128)(2,1)} %bitcast.27), custom_call_target="tpu_custom_call" | custom-call | tf_op jit(solution)/shard_map/stream/pallas_call | solution.py:418
  160.9 0.0 copy-start.2
  160.9 2.4 %copy.32 = bf16[1,1,8,36,2048]{4,2,3,1,0:T(8,128)(2,1)} copy(bf16[1,1,8,36,2048]{4,2,3,1,0:T(8,128)(2,1)} %bitcast.28) | data formatting | bytes 2359296
  163.3 0.0 copy-done.2
  163.3 0.7 copy.33
  (7 shorter events, 0.1 us)
Async XLA Ops:
  0.6 4.4 %copy-start = (bf16[128,768]{1,0:T(8,128)(2,1)S(1)}, bf16[128,768]{1,0:T(8,128)(2,1)}, u32[]{:S(2)}) copy-start(bf16[128,768]{1,0:T(8,128)(2,1)} %param.6) | copy-start | bytes 589828
  4.8 1.4 copy-start.1
  160.9 2.5 %copy-start.2 = (bf16[128,768]{1,0:T(8,128)(2,1)S(1)}, bf16[128,768]{1,0:T(8,128)(2,1)}, u32[]{:S(2)}) copy-start(bf16[128,768]{1,0:T(8,128)(2,1)} %get-tuple-element.9) | copy-start | bytes 589828

commit v4 on v3

--- a/solution.py
+++ b/solution.py
@@ -11,19 +11,9 @@
 UNITS = 128
 
 
-def slot_map(expert_ids, n_expert, slots_cap):
-    flat_ids = expert_ids.reshape(-1)
-    onehot = (flat_ids[:, None] == jnp.arange(n_expert, dtype=jnp.int32)[None, :]).astype(jnp.int32)
-    before = jnp.cumsum(onehot, axis=0) - onehot
-    position = jnp.sum(before * onehot, axis=1)
-    target = position * n_expert + flat_ids
-    placed = target[:, None] == jnp.arange(n_expert * slots_cap, dtype=jnp.int32)[None, :]
-    return placed.reshape(expert_ids.shape[0], expert_ids.shape[1], n_expert * slots_cap)
-
-
-def stream_kernel(nx, nz, ny, pairs_of, select, planes_hbm, gate_hbm, up_hbm, grad_hbm, hid_hbm, tok_out,
-                  stage, wbuf, pairs, planes, spread, rows, scale, grad, hid, acc, bsend, brecv, ysend, yrecv, final, zsend, back,
-                  stage_sem, own_sem, z_send, z_recv, x_send, x_recv, tok_own, tok_send, tok_recv, y_send, y_recv,
+def stream_kernel(nx, nz, ny, pairs_of, ids, weights, tok_hbm, gate_hbm, up_hbm, grad_hbm, hid_hbm, tok_out,
+                  stage, wbuf, pairs, tok, chosen, select, own_planes, planes, spread, rows, scale, grad, hid, acc, bsend, brecv, ysend, yrecv, final, zsend, back,
+                  stage_sem, own_sem, z_send, z_recv, x_send, x_recv, tok_in, tok_own, tok_send, tok_recv, y_send, y_recv,
                   in_sem, p_send, p_recv, hid_sem, hid_send, hid_recv, b_send, b_recv, ys_send, ys_recv,
                   r_own, r_send, r_recv):
     dp, z, y = lax.axis_index("dp"), lax.axis_index("expert"), lax.axis_index("mp")
@@ -41,6 +31,7 @@
     cap = planes.shape[1]
     feat = tok_out.shape[1]
     lanes = feat // 128
+    padded = chosen.shape[0] // nz
     half_units = chunks * UNITS
     bf16, f32 = jnp.bfloat16, jnp.float32
     partner = (dp - c + other, z, y)
@@ -71,8 +62,9 @@
     grad_other = pl.ds(pl.multiple_of(other * half_units, half_units), half_units)
     grad_in = pltpu.make_async_copy(grad_hbm.at[:, grad_cols], grad.at[c], in_sem)
     grad_in.start()
-    plane_in = pltpu.make_async_copy(planes_hbm.at[z], planes.at[z], tok_own)
-    plane_in.start()
+    tokens_in = pltpu.make_async_copy(tok_hbm, tok, tok_in)
+    tokens_in.start()
+    plane_in = pltpu.make_async_copy(own_planes.at[z], planes.at[z], tok_own)
 
     pl.semaphore_wait(barrier, len(peers))
 
@@ -94,10 +86,32 @@
         pltpu.make_async_copy(stage.at[k, c, z], wbuf.at[k, my_block, :], own_sem.at[k]).start()
         return 0
 
+    def dispatch():
+        tokens = tok.shape[0]
+        expert = lax.broadcasted_iota(jnp.int32, (nz, tokens), 0)
+        first, second = ids[0:1, :] == expert, ids[1:2, :] == expert
+        named = jnp.where(first | second, 1.0, 0.0)
+        route = jnp.where(first, weights[0:1, :], 0.0) + jnp.where(second, weights[1:2, :], 0.0)
+        earlier = (lax.broadcasted_iota(jnp.int32, (tokens, tokens), 0)
+                   < lax.broadcasted_iota(jnp.int32, (tokens, tokens), 1))
+        before = jnp.dot(named.astype(bf16), jnp.where(earlier, 1.0, 0.0).astype(bf16), preferred_element_type=f32)
+        place = jnp.where(named > 0.5, before, -1.0).astype(jnp.int32)
+        slot = lax.broadcasted_iota(jnp.int32, (padded, tokens), 0)
+        for e in range(nz):
+            picked = jnp.where(slot == place[e:e + 1, :], 1.0, 0.0)
+            chosen[pl.ds(e * padded, padded), :] = picked.astype(bf16)
+            select[pl.ds(e, cap, stride=nz), :] = picked[:cap]
+            factor = jnp.sum(picked[:cap] * route[e:e + 1, :], axis=1, keepdims=True)
+            own_planes[e, :, feat:] = jnp.broadcast_to(factor, (cap, 128)).astype(bf16)
+        tokens_in.wait()
+        taken = jnp.dot(chosen[...], tok[...], preferred_element_type=f32).astype(bf16)
+        for e in range(nz):
+            own_planes[e, :, :feat] = taken[e * padded:e * padded + cap, :]
+
     def plane_out(o):
         zt = lax.rem(z + o, nz)
         return pltpu.make_async_remote_copy(
-            planes_hbm.at[zt], planes.at[z], tok_send.at[o - 1], tok_recv.at[z], (dp, zt, y), MESH)
+            own_planes.at[zt], planes.at[z], tok_send.at[o - 1], tok_recv.at[z], (dp, zt, y), MESH)
 
     pltpu.make_async_copy(stage.at[0], stage.at[0], stage_sem.at[0]).wait()
     pltpu.make_async_copy(stage.at[0, c, z], wbuf.at[0, my_block, :], own_sem.at[0]).start()
@@ -110,7 +124,9 @@
                 pltpu.make_async_remote_copy(
                     stage.at[0, cc, zt, :, lane], wbuf.at[0, my_block, lane], z_send.at[slot], z_recv.at[slot],
                     (dp - c + cc, zt, y), MESH).start()
+    dispatch()
     lax.fori_loop(1, early, send_z, 0)
+    plane_in.start()
     for o in offsets:
         plane_out(o).start()
     lax.fori_loop(early, chunks, send_z, 0)
@@ -173,7 +189,7 @@
         plane_in.wait()
         for o in offsets:
             zs = lax.rem(z + o, nz)
-            pltpu.make_async_copy(planes_hbm.at[zs], planes.at[zs], tok_recv.at[zs]).wait()
+            pltpu.make_async_copy(own_planes.at[zs], planes.at[zs], tok_recv.at[zs]).wait()
         for j in range(nz):
             for n in range(lanes + 1):
                 spread[n, pl.ds(j, cap, stride=nz), :] = planes[j, :, n * 128:(n + 1) * 128].astype(f32)
@@ -397,19 +413,18 @@
                 spread[m, pl.ds(2 * g * sub + e, per, stride=nz), :] = back[g, e, :, m * 128:(m + 1) * 128].astype(f32)
         rows_g = pl.ds(2 * g * sub, 2 * sub)
         gathered = jnp.concatenate([spread[m, rows_g, :] for m in range(lanes)], axis=1).astype(bf16)
-        result += lax.dot_general(select[rows_g, :], gathered, (((0,), (0,)), ((), ())), preferred_element_type=f32)
+        result += lax.dot_general(select[rows_g, :].astype(bf16), gathered, (((0,), (0,)), ((), ())), preferred_element_type=f32)
     for g in range(pairs_of):
         for o in offsets:
             give_back(g, o).wait_send()
     tok_out[...] = result.astype(bf16)
 
 
-def stream(nx, nz, ny, select, planes, w_gate, w_up, grad):
+def stream(nx, nz, ny, cap, ids, weights, tokens, w_gate, w_up, grad):
     slots, hidden = grad.shape
-    cap = planes.shape[1]
-    feat = planes.shape[2] - 128
+    count, feat = tokens.shape
+    padded = -(-cap // 16) * 16
     d = feat * ny
-    tokens = select.shape[1]
     pairs_of = 3
     chunks = hidden // 2 // UNITS
     part = w_gate.shape[1]
@@ -417,13 +432,17 @@
     dma = pltpu.SemaphoreType.DMA
     return pl.pallas_call(
         functools.partial(stream_kernel, nx, nz, ny, pairs_of),
-        out_shape=(jax.ShapeDtypeStruct((slots, hidden), bf16), jax.ShapeDtypeStruct((tokens, feat), bf16)),
-        in_specs=[pl.BlockSpec(memory_space=pltpu.VMEM)] + [pl.BlockSpec(memory_space=pl.ANY)] * 4,
-        out_specs=(pl.BlockSpec(memory_space=pl.ANY), pl.BlockSpec(memory_space=pltpu.VMEM)),
+        out_shape=(pltpu.VMEM((slots, hidden), bf16), pltpu.VMEM((count, feat), bf16)),
+        in_specs=[pl.BlockSpec(memory_space=pltpu.VMEM)] * 2 + [pl.BlockSpec(memory_space=pl.ANY)] * 4,
+        out_specs=(pl.BlockSpec(memory_space=pltpu.VMEM), pl.BlockSpec(memory_space=pltpu.VMEM)),
         scratch_shapes=[
             pltpu.VMEM((chunks, 2, nz, part, 2 * UNITS), bf16),
             pltpu.VMEM((chunks, d, 2 * UNITS), bf16),
             pltpu.VMEM((2 * slots, 2 * UNITS), bf16),
+            pltpu.VMEM((count, feat), bf16),
+            pltpu.VMEM((nz * padded, count), bf16),
+            pltpu.VMEM((slots, count), f32),
+            pltpu.VMEM((nz, cap, feat + 128), bf16),
             pltpu.VMEM((nz, cap, feat + 128), bf16),
             pltpu.VMEM((feat // 128 + 1, slots, 128), f32),
             pltpu.VMEM((2, slots, d), bf16),
@@ -440,7 +459,7 @@
             pltpu.VMEM((pairs_of, nz, cap // pairs_of, feat), bf16),
             dma((chunks,)), dma((chunks,)), dma((chunks + 1,)), dma((chunks + 1,)),
             dma((4, chunks + 1)), dma((4, chunks + 1)),
-            dma(()), dma((nz - 1,)), dma((nz,)), dma((4,)), dma((4,)),
+            dma(()), dma(()), dma((nz - 1,)), dma((nz,)), dma((4,)), dma((4,)),
             dma(()), dma((6,)), dma((6,)), dma((chunks,)), dma((chunks,)), dma((chunks,)),
             dma((4,)), dma((4,)), dma((6 * pairs_of,)), dma((6 * pairs_of,)),
             dma((pairs_of,)), dma((pairs_of, nz - 1)), dma((pairs_of, nz)),
@@ -448,25 +467,16 @@
         compiler_params=pltpu.CompilerParams(
             collective_id=0, has_side_effects=True, vmem_limit_bytes=62 * 1024 * 1024),
         name="stream",
-    )(select, planes, w_gate, w_up, grad)
+    )(ids, weights, tokens, w_gate, w_up, grad)
 
 
 def per_device(nx, nz, ny, tokens, expert_ids, route_weight, w_gate, w_up, grad_hidden):
     slots_cap = grad_hidden.shape[3]
-    feat = tokens.shape[1]
     hidden_part = w_gate.shape[2]
     slots = nz * slots_cap
-    placed = slot_map(expert_ids, nz, slots_cap).astype(jnp.float32)
-    select = jnp.sum(placed, axis=1)
-    by_expert = select.reshape(-1, slots_cap, nz).transpose(2, 1, 0).reshape(slots, -1)
-    sent_rows = jnp.dot(by_expert.astype(jnp.bfloat16), tokens, preferred_element_type=jnp.float32).astype(jnp.bfloat16)
-    sent_scale = jnp.einsum("tks,tk->s", placed, route_weight.astype(jnp.float32),
-                            precision=lax.Precision.HIGHEST).astype(jnp.bfloat16)
-    sent_scale = sent_scale.reshape(slots_cap, nz).T.reshape(slots)
-    planes = jnp.concatenate([sent_rows, jnp.broadcast_to(sent_scale[:, None], (slots, 128))], axis=1)
-    planes = planes.reshape(nz, slots_cap, feat + 128)
     grad = grad_hidden.transpose(0, 1, 3, 2, 4).reshape(slots, hidden_part)
-    hidden, grad_tokens = stream(nx, nz, ny, select.T.astype(jnp.bfloat16), planes, w_gate, w_up, grad)
+    hidden, grad_tokens = stream(nx, nz, ny, slots_cap, expert_ids.T, route_weight.T.astype(jnp.float32),
+                                 tokens, w_gate, w_up, grad)
     hidden_out = hidden.reshape(1, 1, slots_cap, nz, hidden_part).transpose(0, 1, 3, 2, 4)
     return hidden_out, grad_tokens
 

time: 164 us -> 158 us (0.963)
  local copies, waits for them, and re-layouts: 5.97 us -> 1.69 us
    unnamed x9 -> x2, local copies, waits for them, and re-layouts: 3.97 us -> 1.69 us
where the time goes in v4:
time: 158 us; the launch traced here: 157 us
  Pallas kernels  154 us (97%)
  local copies, waits for them, and re-layouts  1.69 us (1%)
    pallas_call x1, Pallas kernels, stream(): pl.pallas_call(functools.partial(stream_kernel, nx, nz, ny, pairs_of), ou...  154 us

profile of v4, /device:TPU:1, one launch (start us, length us, event | category | flops | bytes accessed | tf_op | source)
XLA Modules:
  0.0 157.5 jit_solution(9523693916063776320)
XLA Ops:
  0.6 1.2 convert_bitcast_fusion.weights
  1.8 153.9 %stream.1 = (bf16[288,2048]{1,0:T(8,128)(2,1)S(1)}, bf16[128,768]{1,0:T(8,128)(2,1)S(1)}) custom-call(s32[2,128]{1,0:T(2,128)} %bitcast.11, f32[2,128]{1,0:T(2,128)} %convert_bitcast_fusion.weights, bf16[128,768]{1,0:T(8,128)(2,1)} %tok_hbm.1, bf16[8,48,2048]{2,1,0:T(8,128)(2,1)} %gate_hbm.1, bf16[8,48,2048]{2,1,0:T(8,128)(2,1)} %up_hbm.1, ...), custom_call_target="tpu_custom_call" | custom-call | tf_op jit(solution)/shard_map/stream/pallas_call | solution.py:433
  155.8 1.0 copy.10
  156.8 0.7 copy.11

commit v5 on v4

--- a/solution.py
+++ b/solution.py
@@ -13,7 +13,7 @@
 
 def stream_kernel(nx, nz, ny, pairs_of, ids, weights, tok_hbm, gate_hbm, up_hbm, grad_hbm, hid_hbm, tok_out,
                   stage, wbuf, pairs, tok, chosen, select, own_planes, planes, spread, rows, scale, grad, hid, acc, bsend, brecv, ysend, yrecv, final, zsend, back,
-                  stage_sem, own_sem, z_send, z_recv, x_send, x_recv, tok_in, tok_own, tok_send, tok_recv, y_send, y_recv,
+                  stage_sem, own_sem, d_send, d_recv, f_send, f_recv, z_send, z_recv, x_send, x_recv, tok_in, tok_own, tok_send, tok_recv, y_send, y_recv,
                   in_sem, p_send, p_recv, hid_sem, hid_send, hid_recv, b_send, b_recv, ys_send, ys_recv,
                   r_own, r_send, r_recv):
     dp, z, y = lax.axis_index("dp"), lax.axis_index("expert"), lax.axis_index("mp")
@@ -76,14 +76,39 @@
         offsets += [o, nz - o]
 
     def send_z(k, _):
-        pltpu.make_async_copy(stage.at[k], stage.at[k], stage_sem.at[k]).wait()
-        for o in offsets + [0]:
+        for o in offsets:
             zt = lax.rem(z + o, nz)
-            for cc in ((c, other) if o else (other,)):
+            for cc in (c, other):
                 pltpu.make_async_remote_copy(
                     stage.at[k, cc, zt], wbuf.at[k, my_block, :], z_send.at[k], z_recv.at[k],
                     (dp - c + cc, zt, y), MESH).start()
+        return 0
+
+    other_block = pl.ds(pl.multiple_of(x * chip_rows + other * own_rows + z * part, 16), part)
+
+    def hand_over(k):
+        return pltpu.make_async_remote_copy(
+            stage.at[k, other, z], wbuf.at[k, my_block, :], d_send.at[k], d_recv.at[k], partner, MESH)
+
+    def ahead(k, way):
+        src = stage.at[k, c, z] if way < 2 else wbuf.at[k, other_block, :]
+        where = my_block if way < 2 else other_block
+        to = right if way % 2 == 0 else left
+        return pltpu.make_async_remote_copy(
+            src, wbuf.at[k, where, :], f_send.at[way, k], f_recv.at[way, k], (to * 2 + c, z, y), MESH)
+
+    def begin(k, _):
+        pltpu.make_async_copy(stage.at[k], stage.at[k], stage_sem.at[k]).wait()
         pltpu.make_async_copy(stage.at[k, c, z], wbuf.at[k, my_block, :], own_sem.at[k]).start()
+        hand_over(k).start()
+        ahead(k, 0).start()
+        ahead(k, 1).start()
+        return 0
+
+    def follow(k, _):
+        hand_over(k).wait_recv()
+        ahead(k, 2).start()
+        ahead(k, 3).start()
         return 0
 
     def dispatch():
@@ -91,7 +116,8 @@
         expert = lax.broadcasted_iota(jnp.int32, (nz, tokens), 0)
         first, second = ids[0:1, :] == expert, ids[1:2, :] == expert
         named = jnp.where(first | second, 1.0, 0.0)
-        route = jnp.where(first, weights[0:1, :], 0.0) + jnp.where(second, weights[1:2, :], 0.0)
+        factors = weights[...].astype(f32)
+        route = jnp.where(first, factors[0:1, :], 0.0) + jnp.where(second, factors[1:2, :], 0.0)
         earlier = (lax.broadcasted_iota(jnp.int32, (tokens, tokens), 0)
                    < lax.broadcasted_iota(jnp.int32, (tokens, tokens), 1))
         before = jnp.dot(named.astype(bf16), jnp.where(earlier, 1.0, 0.0).astype(bf16), preferred_element_type=f32)
@@ -113,18 +139,19 @@
         return pltpu.make_async_remote_copy(
             own_planes.at[zt], planes.at[z], tok_send.at[o - 1], tok_recv.at[z], (dp, zt, y), MESH)
 
-    pltpu.make_async_copy(stage.at[0], stage.at[0], stage_sem.at[0]).wait()
-    pltpu.make_async_copy(stage.at[0, c, z], wbuf.at[0, my_block, :], own_sem.at[0]).start()
+    begin(0, 0)
     for part_of in (0, 1):
         lane = pl.ds(part_of * UNITS, UNITS)
         slot = part_of * chunks
-        for o in offsets + [0]:
+        for o in offsets:
             zt = lax.rem(z + o, nz)
-            for cc in ((c, other) if o else (other,)):
+            for cc in (c, other):
                 pltpu.make_async_remote_copy(
                     stage.at[0, cc, zt, :, lane], wbuf.at[0, my_block, lane], z_send.at[slot], z_recv.at[slot],
                     (dp - c + cc, zt, y), MESH).start()
+    lax.fori_loop(1, chunks, begin, 0)
     dispatch()
+    lax.fori_loop(0, chunks, follow, 0)
     lax.fori_loop(1, early, send_z, 0)
     plane_in.start()
     for o in offsets:
@@ -140,34 +167,66 @@
     def rows_of(chip, first, count):
         return pl.ds(pl.multiple_of(chip * chip_rows + first, 16), count)
 
+    def piece_of(k, part_of):
+        lane = pl.ds(0, 2 * UNITS) if part_of is None else pl.ds(part_of * UNITS, UNITS)
+        slot = k if part_of != 1 else chunks if k == 0 else chunks + 1
+        return lane, slot
+
     def x_copy(k, way, chip, first, count, part_of=None):
-        lane = pl.ds(0, 2 * UNITS) if part_of is None else pl.ds(part_of * UNITS, UNITS)
-        slot = chunks if part_of == 1 else k
+        lane, slot = piece_of(k, part_of)
         where = wbuf.at[k, rows_of(chip, first, count), lane]
         to = right if way % 2 == 0 else left
         return pltpu.make_async_remote_copy(
             where, where, x_send.at[way, slot], x_recv.at[way, slot], (to * 2 + c, z, y), MESH)
 
-    n_in = 2 * nz - 1
+    n_in = 2 * nz - 2
+    runs = []
+    size, base = nz // 2, 0
+    while size:
+        side = lax.rem(z // size, 2)
+        runs.append((base + (1 - side) * size, size))
+        base = base + side * size
+        size //= 2
+
+    def x_start(k, part_of=None):
+        for cc in (0, 1):
+            for at, size in runs:
+                for way in (0, 1):
+                    x_copy(k, way, x, cc * own_rows + at * part, size * part, part_of).start()
+
+    def x_wait(k, sems, way, part_of=None):
+        lane, slot = piece_of(k, part_of)
+        whole = wbuf.at[k, pl.ds(0, n_in * part), lane]
+        pltpu.make_async_copy(whole, whole, sems.at[way, slot]).wait()
 
     def step_own(k):
         whole = wbuf.at[k, pl.ds(0, n_in * part), :]
         pltpu.make_async_copy(whole, whole, z_recv.at[k]).wait()
         pltpu.make_async_copy(stage.at[k, c, z], wbuf.at[k, my_block, :], own_sem.at[k]).wait()
-        x_copy(k, 0, x, 0, chip_rows).start()
-        x_copy(k, 1, x, 0, chip_rows).start()
+        for part_of in ((0, 1) if k == chunks - 1 else (None,)):
+            x_start(k, part_of)
 
     def step_relay(k, part_of=None):
-        x_copy(k, 0, left, 0, chip_rows, part_of).wait_recv()
+        if not part_of:
+            ahead(k, 0).wait_recv()
+            ahead(k, 2).wait_recv()
+        x_wait(k, x_recv, 0, part_of)
         x_copy(k, 2, left, 0, own_rows, part_of).start()
-        x_copy(k, 1, right, 0, chip_rows, part_of).wait_recv()
+        if not part_of:
+            ahead(k, 1).wait_recv()
+            ahead(k, 3).wait_recv()
+        x_wait(k, x_recv, 1, part_of)
         x_copy(k, 3, right, own_rows, own_rows, part_of).start()
 
     def first_own(part_of):
         whole = wbuf.at[0, pl.ds(0, n_in * part), pl.ds(part_of * UNITS, UNITS)]
         pltpu.make_async_copy(whole, whole, z_recv.at[part_of * chunks]).wait()
-        x_copy(0, 0, x, 0, chip_rows, part_of).start()
-        x_copy(0, 1, x, 0, chip_rows, part_of).start()
+        x_start(0, part_of)
+
+    def arrived(k):
+        for part_of in (0, 1):
+            x_copy(k, 2, far, 0, own_rows, part_of).wait_recv()
+            x_copy(k, 3, far, own_rows, own_rows, part_of).wait_recv()
 
     def cols_of(t):
         return pl.ds(pl.multiple_of(t * feat, 128), feat)
@@ -213,7 +272,7 @@
         return pltpu.make_async_remote_copy(bsend.at[n], brecv.at[n], b_send.at[n], b_recv.at[n], partner, MESH)
 
     def compute(k):
-        @pl.when(k > 0)
+        @pl.when((k > 0) & (k < chunks - 1))
         def _():
             x_copy(k, 2, far, 0, own_rows).wait_recv()
             x_copy(k, 3, far, own_rows, own_rows).wait_recv()
@@ -276,9 +335,7 @@
     for n, t in enumerate((y, y_left, y_right, y_far)):
         shared(n, t)
 
-    for part_of in (0, 1):
-        x_copy(0, 2, far, 0, own_rows, part_of).wait_recv()
-        x_copy(0, 3, far, own_rows, own_rows, part_of).wait_recv()
+    arrived(0)
 
     def main(k, _):
         compute(k)
@@ -299,7 +356,12 @@
 
         @pl.when(k == 5)
         def _():
-            step_relay(7)
+            step_relay(7, 0)
+            step_relay(7, 1)
+
+        @pl.when(k == 6)
+        def _():
+            arrived(7)
         return 0
 
     lax.fori_loop(0, chunks, main, 0)
@@ -362,8 +424,8 @@
         keep(g).start()
 
     def sent(k, part_of):
-        x_copy(k, 0, x, 0, chip_rows, part_of).wait_send()
-        x_copy(k, 1, x, 0, chip_rows, part_of).wait_send()
+        x_wait(k, x_send, 0, part_of)
+        x_wait(k, x_send, 1, part_of)
         x_copy(k, 2, left, 0, own_rows, part_of).wait_send()
         x_copy(k, 3, right, own_rows, own_rows, part_of).wait_send()
 
@@ -371,13 +433,20 @@
         whole = wbuf.at[0, pl.ds(0, n_in * part), pl.ds(part_of * UNITS, UNITS)]
         pltpu.make_async_copy(whole, whole, z_send.at[part_of * chunks]).wait()
         sent(0, part_of)
+        sent(chunks - 1, part_of)
 
     def drain(k, _):
         @pl.when(k > 0)
         def _():
             whole = wbuf.at[k, pl.ds(0, n_in * part), :]
             pltpu.make_async_copy(whole, whole, z_send.at[k]).wait()
+
+        @pl.when((k > 0) & (k < chunks - 1))
+        def _():
             sent(k, None)
+        hand_over(k).wait_send()
+        for way in range(4):
+            ahead(k, way).wait_send()
         here, there = hid_out(k)
         here.wait()
         there.wait_send()
@@ -425,7 +494,7 @@
     count, feat = tokens.shape
     padded = -(-cap // 16) * 16
     d = feat * ny
-    pairs_of = 3
+    pairs_of = 9
     chunks = hidden // 2 // UNITS
     part = w_gate.shape[1]
     bf16, f32 = jnp.bfloat16, jnp.float32
@@ -457,8 +526,9 @@
             pltpu.VMEM((feat // 128, slots // pairs_of, 128), f32),
             pltpu.VMEM((pairs_of, nz, cap // pairs_of, feat), bf16),
             pltpu.VMEM((pairs_of, nz, cap // pairs_of, feat), bf16),
-            dma((chunks,)), dma((chunks,)), dma((chunks + 1,)), dma((chunks + 1,)),
-            dma((4, chunks + 1)), dma((4, chunks + 1)),
+            dma((chunks,)), dma((chunks,)), dma((chunks,)), dma((chunks,)), dma((4, chunks)), dma((4, chunks)),
+            dma((chunks + 1,)), dma((chunks + 1,)),
+            dma((4, chunks + 2)), dma((4, chunks + 2)),
             dma(()), dma(()), dma((nz - 1,)), dma((nz,)), dma((4,)), dma((4,)),
             dma(()), dma((6,)), dma((6,)), dma((chunks,)), dma((chunks,)), dma((chunks,)),
             dma((4,)), dma((4,)), dma((6 * pairs_of,)), dma((6 * pairs_of,)),
@@ -475,7 +545,7 @@
     hidden_part = w_gate.shape[2]
     slots = nz * slots_cap
     grad = grad_hidden.transpose(0, 1, 3, 2, 4).reshape(slots, hidden_part)
-    hidden, grad_tokens = stream(nx, nz, ny, slots_cap, expert_ids.T, route_weight.T.astype(jnp.float32),
+    hidden, grad_tokens = stream(nx, nz, ny, slots_cap, expert_ids.T, route_weight.T,
                                  tokens, w_gate, w_up, grad)
     hidden_out = hidden.reshape(1, 1, slots_cap, nz, hidden_part).transpose(0, 1, 3, 2, 4)
     return hidden_out, grad_tokens

time: 158 us -> 150 us (0.949)
  Pallas kernels: 154 us -> 148 us
    pallas_call x1, Pallas kernels: 154 us -> 148 us  [stream(): pl.pallas_call(functools.partial(stream_kernel, nx, nz, ny, pairs_of), ou...]
where the time goes in v5:
time: 150 us
  Pallas kernels  148 us (99%)
  local copies, waits for them, and re-layouts  1.69 us (1%)
    pallas_call x1, Pallas kernels, stream(): pl.pallas_call(functools.partial(stream_kernel, nx, nz, ny, pairs_of), ou...  148 us

profile of v5, /device:TPU:1, one launch (start us, length us, event | category | flops | bytes accessed | tf_op | source)
XLA Modules:
  0.0 150.2 jit_solution(11194169186615690137)
XLA Ops:
  0.6 147.9 %stream.1 = (bf16[288,2048]{1,0:T(8,128)(2,1)S(1)}, bf16[128,768]{1,0:T(8,128)(2,1)S(1)}) custom-call(s32[2,128]{1,0:T(2,128)} %bitcast.10, bf16[2,128]{1,0:T(2,128)(2,1)} %bitcast.11, bf16[128,768]{1,0:T(8,128)(2,1)} %tok_hbm.1, bf16[8,48,2048]{2,1,0:T(8,128)(2,1)} %gate_hbm.1, bf16[8,48,2048]{2,1,0:T(8,128)(2,1)} %up_hbm.1, bf16[288,2048]{1,0:T(8,128)(2,1)} %bitcast.9), custom_call_target="tpu_custom_call" | custom-call | tf_op jit(solution)/shard_map/stream/pallas_call | solution.py:502
  148.5 1.0 copy.10
  149.5 0.7 copy.11

commit v6 on v5

--- a/solution.py
+++ b/solution.py
@@ -150,19 +150,13 @@
                     stage.at[0, cc, zt, :, lane], wbuf.at[0, my_block, lane], z_send.at[slot], z_recv.at[slot],
                     (dp - c + cc, zt, y), MESH).start()
     lax.fori_loop(1, chunks, begin, 0)
-    dispatch()
     lax.fori_loop(0, chunks, follow, 0)
-    lax.fori_loop(1, early, send_z, 0)
-    plane_in.start()
-    for o in offsets:
-        plane_out(o).start()
-    lax.fori_loop(early, chunks, send_z, 0)
+    send_z(1, 0)
 
     def to_partner(n, src, dst):
         return pltpu.make_async_remote_copy(src, dst, p_send.at[n], p_recv.at[n], partner, MESH)
 
     grad_out = to_partner(5, grad_hbm.at[:, grad_other], grad.at[c])
-    grad_out.start()
 
     def rows_of(chip, first, count):
         return pl.ds(pl.multiple_of(chip * chip_rows + first, 16), count)
@@ -271,13 +265,8 @@
     def swap(n):
         return pltpu.make_async_remote_copy(bsend.at[n], brecv.at[n], b_send.at[n], b_recv.at[n], partner, MESH)
 
-    def compute(k):
-        @pl.when((k > 0) & (k < chunks - 1))
-        def _():
-            x_copy(k, 2, far, 0, own_rows).wait_recv()
-            x_copy(k, 3, far, own_rows, own_rows).wait_recv()
+    def activate(k, both):
         at = pl.ds(pl.multiple_of(k * UNITS, UNITS), UNITS)
-        both = jnp.dot(rows[...].reshape(2 * slots, rows.shape[2]), wbuf[k], preferred_element_type=f32)
         gate, up = both[:, :UNITS], both[:, UNITS:]
         weight = scale[...].reshape(2 * slots, UNITS)
         sig = jax.nn.sigmoid(gate)
@@ -292,26 +281,50 @@
         here.start()
         there.start()
 
-        def backward(n, _):
-            cols = cols_of(lax.rem(y + 2 + 3 * n + 3 * (n // 2) + 2 * (n // 3), ny))
-            term = lax.dot_general(pairs[...], wbuf[k, cols, :], (((1,), (1,)), ((), ())), preferred_element_type=f32)
-            acc[:, :, cols] += term.reshape(2, slots, feat)
-
-            @pl.when(k == chunks - 1)
-            def _():
-                bsend[n] = acc[other, :, cols].astype(bf16)
-                swap(n).start()
+    def backward(k, n):
+        cols = cols_of(lax.rem(y + 2 + 3 * n + 3 * (n // 2) + 2 * (n // 3), ny))
+        term = lax.dot_general(pairs[...], wbuf[k, cols, :], (((1,), (1,)), ((), ())), preferred_element_type=f32)
+        acc[:, :, cols] += term.reshape(2, slots, feat)
+        return cols
+
+    def backward_step(k):
+        def step(n, _):
+            backward(k, n)
             return 0
-
-        lax.fori_loop(0, ny, backward, 0)
-
-    acc[...] = jnp.zeros_like(acc)
+        return step
+
+    def backward_last(n, _):
+        cols = backward(chunks - 1, n)
+        bsend[n] = acc[other, :, cols].astype(bf16)
+        swap(n).start()
+        return 0
+
+    def compute(k):
+        @pl.when(k > 0)
+        def _():
+            x_copy(k, 2, far, 0, own_rows).wait_recv()
+            x_copy(k, 3, far, own_rows, own_rows).wait_recv()
+        activate(k, jnp.dot(rows[...].reshape(2 * slots, rows.shape[2]), wbuf[k], preferred_element_type=f32))
+        lax.fori_loop(0, ny, backward_step(k), 0)
+
+    def forward_part(k, chip):
+        which = pl.ds(pl.multiple_of(chip * chip_rows, 128), chip_rows)
+        return jnp.dot(rows[:, :, which].reshape(2 * slots, chip_rows), wbuf[k, which, :], preferred_element_type=f32)
+
+    dispatch()
     pltpu.make_async_copy(stage.at[0, c, z], wbuf.at[0, my_block, :], own_sem.at[0]).wait()
     first_own(0)
     first_own(1)
+    lax.fori_loop(2, early, send_z, 0)
+    plane_in.start()
+    for o in offsets:
+        plane_out(o).start()
     step_relay(0, 0)
     step_relay(0, 1)
     step_own(1)
+    lax.fori_loop(early, chunks, send_z, 0)
+    grad_out.start()
+    acc[...] = jnp.zeros_like(acc)
     step_own(2)
     step_relay(1)
     step_own(3)
@@ -358,13 +371,13 @@
         def _():
             step_relay(7, 0)
             step_relay(7, 1)
-
-        @pl.when(k == 6)
-        def _():
-            arrived(7)
-        return 0
-
-    lax.fori_loop(0, chunks, main, 0)
+        return 0
+
+    lax.fori_loop(0, chunks - 1, main, 0)
+    last = chunks - 1
+    near = forward_part(last, x) + forward_part(last, left) + forward_part(last, right)
+    arrived(last)
+    activate(last, near + forward_part(last, far))
 
     subs = 2 * pairs_of
     sub = slots // subs
@@ -390,9 +403,11 @@
         rows_n = pl.ds(n * sub, sub)
         return acc[c, rows_n, cols_of(swaps[order])] + brecv[order, rows_n].astype(f32)
 
+    lax.fori_loop(0, 2, backward_last, 0)
     swap(0).wait_recv()
     for n in range(subs):
         pass_on(0, n, mine(0, n))
+    lax.fori_loop(2, ny, backward_last, 0)
     swap(1).wait_recv()
     swap(2).wait_recv()
     for g in range(pairs_of):
@@ -410,6 +425,16 @@
     def keep(g):
         return pltpu.make_async_copy(zsend.at[g, z], back.at[g, z], r_own.at[g])
 
+    def absorb(g):
+        keep(g).wait()
+        for o in offsets:
+            zs = lax.rem(z + o, nz)
+            pltpu.make_async_copy(zsend.at[g, zs], back.at[g, zs], r_recv.at[g, zs]).wait()
+        for e in range(nz):
+            for m in range(lanes):
+                spread[m, pl.ds(2 * g * sub + e, per, stride=nz), :] = back[g, e, :, m * 128:(m + 1) * 128].astype(f32)
+
+    behind = 4
     for g in range(pairs_of):
         for i in (0, 1):
             n = 2 * g + i
@@ -422,6 +447,8 @@
         for o in offsets:
             give_back(g, o).start()
         keep(g).start()
+        if g >= behind:
+            absorb(g - behind)
 
     def sent(k, part_of):
         x_wait(k, x_send, 0, part_of)
@@ -471,22 +498,14 @@
         for n in range(subs):
             piece(kind, n).wait_send()
 
-    result = jnp.zeros(tok_out.shape, f32)
-    for g in range(pairs_of):
-        keep(g).wait()
-        for o in offsets:
-            zs = lax.rem(z + o, nz)
-            pltpu.make_async_copy(zsend.at[g, zs], back.at[g, zs], r_recv.at[g, zs]).wait()
-        for e in range(nz):
-            for m in range(lanes):
-                spread[m, pl.ds(2 * g * sub + e, per, stride=nz), :] = back[g, e, :, m * 128:(m + 1) * 128].astype(f32)
-        rows_g = pl.ds(2 * g * sub, 2 * sub)
-        gathered = jnp.concatenate([spread[m, rows_g, :] for m in range(lanes)], axis=1).astype(bf16)
-        result += lax.dot_general(select[rows_g, :].astype(bf16), gathered, (((0,), (0,)), ((), ())), preferred_element_type=f32)
+    for g in range(pairs_of - behind, pairs_of):
+        absorb(g)
+    gathered = jnp.concatenate([spread[m] for m in range(lanes)], axis=1).astype(bf16)
+    tok_out[...] = lax.dot_general(select[...].astype(bf16), gathered, (((0,), (0,)), ((), ())),
+                                   preferred_element_type=f32).astype(bf16)
     for g in range(pairs_of):
         for o in offsets:
             give_back(g, o).wait_send()
-    tok_out[...] = result.astype(bf16)
 
 
 def stream(nx, nz, ny, cap, ids, weights, tokens, w_gate, w_up, grad):

time: 150 us -> 150 us (level)
  no operation moved by 1% of the time
where the time goes in v6:
time: 150 us
  Pallas kernels  148 us (99%)
  local copies, waits for them, and re-layouts  1.69 us (1%)
    pallas_call x1, Pallas kernels, stream(): pl.pallas_call(functools.partial(stream_kernel, nx, nz, ny, pairs_of), ou...  148 us

profile of v6, /device:TPU:1, one launch (start us, length us, event | category | flops | bytes accessed | tf_op | source)
XLA Modules:
  0.0 149.9 jit_solution(1129385399631429963)
XLA Ops:
  0.6 147.6 %stream.1 = (bf16[288,2048]{1,0:T(8,128)(2,1)S(1)}, bf16[128,768]{1,0:T(8,128)(2,1)S(1)}) custom-call(s32[2,128]{1,0:T(2,128)} %bitcast.10, bf16[2,128]{1,0:T(2,128)(2,1)} %bitcast.11, bf16[128,768]{1,0:T(8,128)(2,1)} %tok_hbm.1, bf16[8,48,2048]{2,1,0:T(8,128)(2,1)} %gate_hbm.1, bf16[8,48,2048]{2,1,0:T(8,128)(2,1)} %up_hbm.1, bf16[288,2048]{1,0:T(8,128)(2,1)} %bitcast.9), custom_call_target="tpu_custom_call" | custom-call | tf_op jit(solution)/shard_map/stream/pallas_call | solution.py:521
  148.2 1.0 copy.10
  149.2 0.7 copy.11
